TPU v7x, 512 devices: a whole 4x8x8 slice. The times are simulated.
512 devices in a mesh: lat: 16 (over y, core), lon: 32 (over x, z).
Axes of the slice: x: 4, y: 8, z: 8, core: 2. Of those that a mesh axis runs over, the one named last changes fastest.
Arguments:
- latent: bfloat16 [32, 384, 640], P('lat', 'lon'), may hold values from -6 to 6
- lon_filter: bfloat16 [9, 384], replicated, may hold values from -0.3125 to 0.3125
- mix_weight: bfloat16 [9, 640, 20], P(None, 'lon'), may hold values from -1.25 to 1.25
- band_weight: bfloat16 [9, 32, 3], P(None, 'lat'), may hold values from -1.25 to 1.25
- offsets: int32 [32], P('lat'), may hold values from -2 to 31, as said below
- w_up: bfloat16 [640, 1280], replicated, may hold values from -0.25 to 0.25
- w_down: bfloat16 [1280, 640], replicated, may hold values from -0.15625 to 0.15625
Outputs:
- result: bfloat16 [32, 384, 640], P('lat', 'lon')
Inputs may be any that keep to these rules, and one draw needn't show every extreme that they name: offsets[i] - i lies between -2 and 0, so a band's rows lie within 2 rows of its output row; in every aligned block of 2 rows the first row's band starts 2 rows below it and the last row's band ends 2 rows above it.
All inputs are finite; a program needn't handle non-finite values.
Results may differ from a plain program's by a relative error of at most 0.0095.
Values may be sent and summed in bfloat16 or wider, within the bound.
A program may use at most 128 MiB of HBM per device.

v0:
```python
import jax
import jax.numpy as jnp
from jax import lax
from jax.sharding import PartitionSpec as P

BW = 3
REACH = 2


def extended(block, sides, width):
    for axis, dim in sides:
        count = lax.axis_size(axis)
        forward = [(i, i + 1) for i in range(count - 1)]
        backward = [(target, source) for source, target in forward]
        low = lax.ppermute(
            lax.slice_in_dim(block, block.shape[dim] - width, None, axis=dim), axis, forward
        )
        high = lax.ppermute(lax.slice_in_dim(block, 0, width, axis=dim), axis, backward)
        block = jnp.concatenate([low, block, high], axis=dim)
    return block


def circulant(lon_filter):
    length = lon_filter.shape[1]
    places = jnp.arange(length, dtype=jnp.int32)
    index_table = (places[:, None] - places[None, :]) % length
    return lon_filter[:, index_table]


def block_mix(mix_weight):
    chan_width = mix_weight.shape[1]
    group_size = mix_weight.shape[2]
    repeated = jnp.tile(mix_weight.astype(jnp.float32), (1, 1, chan_width // group_size))
    member = jnp.arange(chan_width, dtype=jnp.int32) // group_size
    same_group = (member[:, None] == member[None, :]).astype(jnp.float32)
    return repeated * same_group[None]


def feed_forward(summed, w_up, w_down):
    flat_rows = summed.reshape(-1, summed.shape[-1]).astype(jnp.float32)
    row_mean = jnp.mean(flat_rows, axis=1, keepdims=True)
    centred = flat_rows - row_mean
    row_var = jnp.mean(centred * centred, axis=1, keepdims=True)
    normed = (centred * lax.rsqrt(row_var + 1e-05)).astype(jnp.bfloat16)
    hidden = jax.nn.gelu(
        jnp.dot(normed, w_up, preferred_element_type=jnp.float32), approximate=False
    ).astype(jnp.bfloat16)
    output = flat_rows + jnp.dot(hidden, w_down, preferred_element_type=jnp.float32)
    return output.astype(jnp.bfloat16).reshape(summed.shape)


def local(latent, lon_filter, mix_weight, band_weight, offsets, w_up, w_down):
    lat_dev = latent.shape[0]
    grouped = lax.all_to_all(latent, "lon", split_axis=2, concat_axis=1, tiled=True)
    lon_table = circulant(lon_filter)
    mix_blocks = block_mix(mix_weight)
    spread = lax.dot_general(
        grouped, lon_table, (((1,), (2,)), ((), ())), preferred_element_type=jnp.float32
    )
    mixed_rows = extended(
        jnp.einsum("rckx,kdc->rkdx", spread, mix_blocks, precision=lax.Precision.HIGHEST).astype(
            jnp.bfloat16
        ),
        (("lat", 0),),
        REACH,
    )
    first_row = lax.axis_index("lat") * lat_dev
    rim_span = lat_dev + 2 * REACH
    positions = offsets[:, None] + jnp.arange(BW, dtype=jnp.int32)[None, :] - first_row + REACH
    onehot = (positions[:, :, None] == jnp.arange(rim_span, dtype=jnp.int32)[None, None, :]).astype(
        jnp.float32
    )
    band_dense = jnp.einsum(
        "kit,itr->kir", band_weight.astype(jnp.float32), onehot, precision=lax.Precision.HIGHEST
    ).astype(jnp.bfloat16)
    convolved = jnp.einsum(
        "kir,rkdx->idx", band_dense, mixed_rows, preferred_element_type=jnp.float32
    ).astype(jnp.bfloat16)
    returned = lax.all_to_all(convolved, "lon", split_axis=2, concat_axis=1, tiled=True)
    turned = jnp.transpose(returned, (0, 2, 1)).astype(jnp.float32)
    summed = (latent.astype(jnp.float32) + turned).astype(jnp.bfloat16)
    return feed_forward(summed, w_up, w_down)


def solution(mesh):
    return jax.shard_map(
        local,
        mesh=mesh,
        in_specs=(
            P("lat", "lon", None),
            P(),
            P(None, "lon", None),
            P(None, "lat", None),
            P("lat"),
            P(),
            P(),
        ),
        out_specs=P("lat", "lon", None),
        check_vma=False,
    )
```

profile of v0, /device:TPU:25, one launch (start us, length us, event | category | flops | bytes accessed | tf_op | source)
XLA Modules:
  0.0 600.0 jit_solution(667034243852616495)
XLA Ops:
  0.0 1.1 copy.56
  1.1 0.9 reshape.178
  2.0 12.9 %all-to-all-start = ((bf16[32,2,240]{2,1,0:T(2,128)(2,1)}), bf16[32,2,240]{2,1,0:T(2,128)(2,1)S(1)}, u32[]{:S(2)}, u32[]{:S(2)}) async-start(bf16[32,2,240]{2,1,0:T(2,128)(2,1)} %reshape.178), calls=%async_computation | async-start | bytes 65536 | tf_op jit(solution)/shard_map/all_to_all | solution.py:54
  14.9 0.3 compare_select_fusion
  15.6 510.6 %gather_fusion = bf16[147456,9]{1,0:T(8,128)(2,1)} fusion(bf16[9,384]{0,1:T(8,128)(2,1)S(1)} %copy.54, s32[147456]{0:T(1024)S(1)} %broadcast_clamp_fusion), kind=kCustom, calls=%fused_computation | custom fusion | bytes 5898240 | tf_op jit(solution)/shard_map/gather | solution.py:27
  526.2 29.5 %copy.55 = bf16[384,384,9]{1,0,2:T(8,128)(2,1)} copy(bf16[384,384,9]{2,1,0:T(8,128)(2,1)} %bitcast.64) | data formatting | bytes 5308416 | tf_op jit(solution)/shard_map/gather | solution.py:27
  555.7 0.3 reshape.179
  556.1 0.5 all_to_all.23
  556.6 2.9 fusion.4
  559.6 0.7 fusion.7
  560.2 5.3 collective-permute-start
  565.5 1.9 collective-permute-start.1
  567.5 0.3 fusion.15
  567.8 1.8 collective-permute-done
  569.5 5.6 collective-permute-done.1
  575.3 0.7 fusion.12
  576.0 0.2 copy.62
  576.2 0.2 reshape.180
  576.4 18.0 %all_to_all.27 = bf16[32,2,240]{2,1,0:T(2,128)(2,1)S(1)} all-to-all(bf16[32,2,240]{2,1,0:T(2,128)(2,1)S(1)} %reshape.180), channel_id=1, replica_groups=mesh['lat'=16,'lon'=32] {'lon'}, dimensions={0} | all-to-all | bytes 61440 | tf_op jit(solution)/shard_map/all_to_all | solution.py:79
  594.8 0.7 reshape.163
  595.5 0.6 copy.64
  596.1 0.3 reshape.162
  597.2 2.2 fusion.11
  599.4 0.6 copy.69
  (34 shorter events, 1.7 us)
Async XLA Ops:
  0.0 597.1 %copy-start = (bf16[1280,640]{1,0:T(8,128)(2,1)S(1)}, bf16[1280,640]{1,0:T(8,128)(2,1)}, u32[]{:S(2)}) copy-start(bf16[1280,640]{1,0:T(8,128)(2,1)} %param.13) | copy-start | bytes 4915204
  1.1 14.4 %copy-start.3 = (bf16[9,384]{1,0:T(8,128)(2,1)S(1)}, bf16[9,384]{1,0:T(8,128)(2,1)}, u32[]{:S(2)}) copy-start(bf16[9,384]{1,0:T(8,128)(2,1)} %param.8) | copy-start | bytes 20740
  2.0 553.7 %all-to-all-start = ((bf16[32,2,240]{2,1,0:T(2,128)(2,1)}), bf16[32,2,240]{2,1,0:T(2,128)(2,1)S(1)}, u32[]{:S(2)}, u32[]{:S(2)}) async-start(bf16[32,2,240]{2,1,0:T(2,128)(2,1)} %reshape.178), calls=%async_computation | async-start | bytes 65536 | tf_op jit(solution)/shard_map/all_to_all | solution.py:54
  556.6 3.0 copy-start.2
  556.6 10.9 %copy-start.4 = (s32[2]{0:T(128)S(1)}, s32[2]{0:T(128)}, u32[]{:S(2)}) copy-start(s32[2]{0:T(128)} %param.11) | copy-start | bytes 28
  556.6 10.9 %copy-start.5 = (bf16[9,2,3]{0,1,2:T(2,128)(2,1)S(1)}, bf16[9,2,3]{0,1,2:T(2,128)(2,1)}, u32[]{:S(2)}) copy-start(bf16[9,2,3]{0,1,2:T(2,128)(2,1)} %param.10) | copy-start | bytes 328
  560.2 9.3 %collective-permute-start = (bf16[2,9,20,384]{3,2,0,1:T(8,128)(2,1)S(1)}, bf16[2,9,20,384]{3,2,0,1:T(8,128)(2,1)S(1)}, u32[]{:S(2)}, u32[]{:S(2)}) collective-permute-start(bf16[2,9,20,384]{3,2,0,1:T(8,128)(2,1)S(1)} %fusion.7), channel_id=1, source_target_pairs={{0,32},{32,64},{64,96},{96,128},{128,160},{160,192},{192,224},{224... | collective-permute-start | bytes 829448 | tf_op jit(solution)/shard_map/ppermute | solution.py:15
  565.5 9.6 %collective-permute-start.1 = (bf16[2,9,20,384]{3,2,0,1:T(8,128)(2,1)S(1)}, bf16[2,9,20,384]{3,2,0,1:T(8,128)(2,1)S(1)}, u32[]{:S(2)}, u32[]{:S(2)}) collective-permute-start(bf16[2,9,20,384]{3,2,0,1:T(8,128)(2,1)S(1)} %fusion.7), channel_id=1, source_target_pairs={{32,0},{64,32},{96,64},{128,96},{160,128},{192,160},{224,192},{256... | collective-permute-start | bytes 829448 | tf_op jit(solution)/shard_map/ppermute | solution.py:18
  576.0 20.4 %copy-start.1 = (bf16[2,12,640]{2,0,1:T(2,128)(2,1)S(1)}, bf16[2,12,640]{2,0,1:T(2,128)(2,1)}, u32[]{:S(2)}) copy-start(bf16[2,12,640]{2,0,1:T(2,128)(2,1)} %param.7) | copy-start | bytes 92164
where the time goes:
time: 601 us; the launch traced here: 600 us
  local copies, waits for them, and re-layouts  547 us (91%)
  starting transfers between devices  20.1 us (3%)
  blocking collectives  18 us (3%)
  waiting for transfers between devices  7.37 us (1%)
  matrix products  6.72 us (1%)
    gather x2, local copies, waits for them, and re-layouts, circulant(): return lon_filter[:, index_table]  540 us
    all_to_all x1, blocking collectives, local(): lax.all_to_all(convolved, 'lon', split_axis=2, concat_axis=1, tiled=True)  18 us
    all_to_all x1, starting transfers between devices, local(): lax.all_to_all(latent, 'lon', split_axis=2, concat_axis=1, tiled=True)  12.9 us
  transfers between devices with their start and end apart: 3, of which 2 were waited for; matrix products, arithmetic and copies ran while one was open for 90% of the time, Pallas kernels for 0%

commit v1 on v0

--- a/solution.py
+++ b/solution.py
@@ -1,6 +1,8 @@
 import jax
 import jax.numpy as jnp
 from jax import lax
+from jax.experimental import pallas as pl
+from jax.experimental.pallas import tpu as pltpu
 from jax.sharding import PartitionSpec as P
 
 BW = 3
@@ -20,11 +22,21 @@
     return block
 
 
+def circulant_kernel(filter_ref, table_ref):
+    length = filter_ref.shape[1]
+    for k in range(filter_ref.shape[0]):
+        row = filter_ref[k : k + 1, :].astype(jnp.float32)
+        spread_row = jnp.broadcast_to(row, (length, length))
+        turned = pltpu.roll(spread_row, 0, 1, stride=1, stride_axis=0)
+        table_ref[k] = turned.astype(jnp.bfloat16)
+
+
 def circulant(lon_filter):
-    length = lon_filter.shape[1]
-    places = jnp.arange(length, dtype=jnp.int32)
-    index_table = (places[:, None] - places[None, :]) % length
-    return lon_filter[:, index_table]
+    count, length = lon_filter.shape
+    return pl.pallas_call(
+        circulant_kernel,
+        out_shape=jax.ShapeDtypeStruct((count, length, length), jnp.bfloat16),
+    )(lon_filter)
 
 
 def block_mix(mix_weight):
@@ -55,7 +67,7 @@
     lon_table = circulant(lon_filter)
     mix_blocks = block_mix(mix_weight)
     spread = lax.dot_general(
-        grouped, lon_table, (((1,), (2,)), ((), ())), preferred_element_type=jnp.float32
+        grouped, lon_table, (((1,), (1,)), ((), ())), preferred_element_type=jnp.float32
     )
     mixed_rows = extended(
         jnp.einsum("rckx,kdc->rkdx", spread, mix_blocks, precision=lax.Precision.HIGHEST).astype(

time: 601 us -> 62.5 us (0.10)
  local copies, waits for them, and re-layouts: 547 us -> 6.29 us
  blocking collectives: 18 us -> 11.7 us
  waiting for transfers between devices: 7.37 us -> 13.4 us
    gather x2 -> x0, local copies, waits for them, and re-layouts: 540 us -> none  [circulant(): return lon_filter[:, index_table]]
    all_to_all x1, blocking collectives: 18 us -> 11.7 us  [local(): lax.all_to_all(convolved, 'lon', split_axis=2, concat_axis=1, tiled=True)]
    all_to_all x1, waiting for transfers between devices: 0.01 us -> 6.04 us  [local(): lax.all_to_all(latent, 'lon', split_axis=2, concat_axis=1, tiled=True)]
  transfers between devices with their start and end apart: 3 -> 3, of which waited for: 2 -> 3; matrix products, arithmetic and copies ran while one was open for 90% -> 1% of each run, Pallas kernels for 0% -> 4%
where the time goes in v1:
time: 62.5 us; the launch traced here: 62.1 us
  starting transfers between devices  21.2 us (34%)
  waiting for transfers between devices  13.4 us (21%)
  blocking collectives  11.7 us (19%)
  local copies, waits for them, and re-layouts  6.29 us (10%)
  matrix products  6.1 us (10%)
  Pallas kernels  2.58 us (4%)
  other arithmetic  0.64 us (1%)
    all_to_all x1, starting transfers between devices, local(): lax.all_to_all(latent, 'lon', split_axis=2, concat_axis=1, tiled=True)  12.9 us
    all_to_all x1, blocking collectives, local(): lax.all_to_all(convolved, 'lon', split_axis=2, concat_axis=1, tiled=True)  11.7 us
    ppermute x1, starting transfers between devices, extended(): lax.ppermute(lax.slice_in_dim(block, block.shape[dim] - width, None, axis...  6.43 us
    all_to_all x1, waiting for transfers between devices, local(): lax.all_to_all(latent, 'lon', split_axis=2, concat_axis=1, tiled=True)  6.04 us
    ppermute x1, waiting for transfers between devices, extended(): lax.ppermute(lax.slice_in_dim(block, 0, width, axis=dim), axis, backward)  5.61 us
    unnamed x17, local copies, waits for them, and re-layouts  2.9 us
    pallas_call x1, Pallas kernels, circulant(): pl.pallas_call(circulant_kernel, out_shape=jax.ShapeDtypeStruct((count, l...  2.58 us
    dot_general x1, matrix products, local(): lax.dot_general(grouped, lon_table, (((1,), (1,)), ((), ())), preferred_e...  2.31 us
  transfers between devices with their start and end apart: 3, of which 3 were waited for; matrix products, arithmetic and copies ran while one was open for 1% of the time, Pallas kernels for 4%

profile of v1, /device:TPU:25, one launch (start us, length us, event | category | flops | bytes accessed | tf_op | source)
XLA Modules:
  0.0 62.1 jit_solution(17716540634547029613)
XLA Ops:
  0.0 1.1 %copy.48 = bf16[2,12,640]{1,0,2:T(2,128)(2,1)S(1)} copy(bf16[2,12,640]{2,0,1:T(2,128)(2,1)} %param.7) | data formatting | bytes 61440 | tf_op args[0]
  1.1 0.9 %reshape.126 = bf16[32,2,240]{2,1,0:T(2,128)(2,1)} reshape(bf16[640,2,12]{2,1,0:T(2,128)(2,1)S(1)} %bitcast.58) | data formatting | bytes 61440
  2.0 12.9 %all-to-all-start = ((bf16[32,2,240]{2,1,0:T(2,128)(2,1)}), bf16[32,2,240]{2,1,0:T(2,128)(2,1)S(1)}, u32[]{:S(2)}, u32[]{:S(2)}) async-start(bf16[32,2,240]{2,1,0:T(2,128)(2,1)} %reshape.126), calls=%async_computation | async-start | bytes 65536 | tf_op jit(solution)/shard_map/all_to_all | solution.py:66
  15.0 2.6 %shard_map.73 = bf16[9,384,384]{2,1,0:T(8,128)(2,1)} custom-call(bf16[9,384]{1,0:T(8,128)(2,1)} %filter_ref.1), custom_call_target="tpu_custom_call" | custom-call | tf_op jit(solution)/shard_map/pallas_call | solution.py:36
  17.6 6.0 %all-to-all-done = bf16[32,2,240]{2,1,0:T(2,128)(2,1)S(1)} async-done(((bf16[32,2,240]{2,1,0:T(2,128)(2,1)}), bf16[32,2,240]{2,1,0:T(2,128)(2,1)S(1)}, u32[]{:S(2)}, u32[]{:S(2)}) %all-to-all-start) | async-done | bytes 30752 | tf_op jit(solution)/shard_map/all_to_all | solution.py:66
  23.6 0.3 reshape.127
  24.0 0.5 all_to_all.23
  24.5 2.3 %fusion = f32[2,20,9,384]{3,1,0,2:T(8,128)S(1)} fusion(bf16[9,384,384]{2,1,0:T(8,128)(2,1)} %shard_map.73, bf16[2,384,20]{1,0,2:T(2,128)(2,1)S(1)} %all_to_all.23), kind=kOutput, calls=%fused_computation | convolution fusion | flops 106168320 | bytes 3237888 | tf_op jit(solution)/shard_map/dot_general | solution.py:69
  26.8 0.7 %fusion.4 = bf16[2,9,20,384]{3,2,0,1:T(8,128)(2,1)S(1)} fusion(f32[2,20,9,384]{3,1,0,2:T(8,128)S(1)} %fusion, bf16[9,20,20]{2,1,0:T(8,128)(2,1)S(1)} %copy-done.2, f32[20,20]{1,0:T(8,128)S(1)} %compare_convert_fusion), kind=kOutput, calls=%fused_computation.5 | convolution fusion | flops 33323040 | bytes 838240 | tf_op jit(solution)/shard_map/rckx,kdc->rkdx/dot_general | solution.py:73
  27.5 6.4 %collective-permute-start = (bf16[2,9,20,384]{3,2,0,1:T(8,128)(2,1)S(1)}, bf16[2,9,20,384]{3,2,0,1:T(8,128)(2,1)S(1)}, u32[]{:S(2)}, u32[]{:S(2)}) collective-permute-start(bf16[2,9,20,384]{3,2,0,1:T(8,128)(2,1)S(1)} %fusion.4), channel_id=1, source_target_pairs={{0,32},{32,64},{64,96},{96,128},{128,160},{160,192},{192,224},{224... | collective-permute-start | bytes 829448 | tf_op jit(solution)/shard_map/ppermute | solution.py:17
  34.0 1.9 %collective-permute-start.1 = (bf16[2,9,20,384]{3,2,0,1:T(8,128)(2,1)S(1)}, bf16[2,9,20,384]{3,2,0,1:T(8,128)(2,1)S(1)}, u32[]{:S(2)}, u32[]{:S(2)}) collective-permute-start(bf16[2,9,20,384]{3,2,0,1:T(8,128)(2,1)S(1)} %fusion.4), channel_id=1, source_target_pairs={{32,0},{64,32},{96,64},{128,96},{160,128},{192,160},{224,192},{256... | collective-permute-start | bytes 829448 | tf_op jit(solution)/shard_map/ppermute | solution.py:20
  36.0 0.3 fusion.12
  36.2 1.8 %collective-permute-done = bf16[2,9,20,384]{3,2,0,1:T(8,128)(2,1)S(1)} collective-permute-done((bf16[2,9,20,384]{3,2,0,1:T(8,128)(2,1)S(1)}, bf16[2,9,20,384]{3,2,0,1:T(8,128)(2,1)S(1)}, u32[]{:S(2)}, u32[]{:S(2)}) %collective-permute-start) | collective-permute-done | bytes 276512 | tf_op jit(solution)/shard_map/ppermute | solution.py:17
  38.0 5.6 %collective-permute-done.1 = bf16[2,9,20,384]{3,2,0,1:T(8,128)(2,1)S(1)} collective-permute-done((bf16[2,9,20,384]{3,2,0,1:T(8,128)(2,1)S(1)}, bf16[2,9,20,384]{3,2,0,1:T(8,128)(2,1)S(1)}, u32[]{:S(2)}, u32[]{:S(2)}) %collective-permute-start.1) | collective-permute-done | bytes 276512 | tf_op jit(solution)/shard_map/ppermute | solution.py:20
  43.8 0.7 %fusion.9 = bf16[2,20,384]{2,0,1:T(2,128)(2,1)S(1)} fusion(bf16[6,9,20,384]{3,2,0,1:T(8,128)(2,1)S(1)} %pad_maximum_fusion, bf16[9,2,6]{0,2,1:T(8,128)(2,1)S(1)} %fusion.12), kind=kOutput, calls=%fused_computation.9 | convolution fusion | flops 1674240 | bytes 860376 | tf_op jit(solution)/shard_map/kir,rkdx->idx/dot_general | solution.py:88
  44.5 0.2 copy.54
  44.7 0.2 reshape.128
  44.9 11.7 %all_to_all.27 = bf16[32,2,240]{2,1,0:T(2,128)(2,1)S(1)} all-to-all(bf16[32,2,240]{2,1,0:T(2,128)(2,1)S(1)} %reshape.128), channel_id=1, replica_groups=mesh['lat'=16,'lon'=32] {'lon'}, dimensions={0} | all-to-all | bytes 61440 | tf_op jit(solution)/shard_map/all_to_all | solution.py:91
  56.6 0.2 reshape.129
  56.9 0.7 %reshape.120 = f32[2,20,32,12]{3,2,0,1:T(8,128)S(1)} reshape(bf16[2,20,384]{2,0,1:T(2,128)(2,1)S(1)} %copy.55) | data formatting | bytes 92160 | tf_op jit(solution)/shard_map/convert_element_type | solution.py:92
  57.6 0.6 %copy.56 = f32[2,32,20,12]{2,1,0,3:T(8,128)S(1)} copy(f32[2,32,20,12]{3,1,0,2:T(8,128)S(1)} %bitcast.55) | data formatting | bytes 122880 | tf_op jit(solution)/shard_map/convert_element_type | solution.py:92
  58.3 0.3 reshape.119
  59.3 2.2 %fusion.8 = bf16[24,640]{1,0:T(8,128)(2,1)S(1)} fusion(f32[24,640]{1,0:T(8,128)S(1)} %reshape.118, bf16[1280,640]{1,0:T(8,128)(2,1)S(1)} %copy-done, bf16[640,1280]{1,0:T(8,128)(2,1)} %param.12, f32[24]{0:T(128)S(1)} %rsqrt.12, f32[24]{0:T(128)S(1)} %div.24), kind=kOutput, calls=%fused_computation.8 | convolution fusion | flops 80716800 | bytes 3369152 | tf_op jit(solution)/shard_map/dot_general | solution.py:60
  61.5 0.6 %copy.61 = bf16[2,12,640]{2,0,1:T(2,128)(2,1)} copy(bf16[2,12,640]{2,1,0:T(8,128)(2,1)S(1)} %reshape.117) | data formatting | bytes 61440 | tf_op jit(solution)/shard_map/reshape | solution.py:61
  (27 shorter events, 1.3 us)
Async XLA Ops:
  0.0 59.3 %copy-start = (bf16[1280,640]{1,0:T(8,128)(2,1)S(1)}, bf16[1280,640]{1,0:T(8,128)(2,1)}, u32[]{:S(2)}) copy-start(bf16[1280,640]{1,0:T(8,128)(2,1)} %param.13) | copy-start | bytes 4915204
  2.0 21.6 %all-to-all-start = ((bf16[32,2,240]{2,1,0:T(2,128)(2,1)}), bf16[32,2,240]{2,1,0:T(2,128)(2,1)S(1)}, u32[]{:S(2)}, u32[]{:S(2)}) async-start(bf16[32,2,240]{2,1,0:T(2,128)(2,1)} %reshape.126), calls=%async_computation | async-start | bytes 65536 | tf_op jit(solution)/shard_map/all_to_all | solution.py:66
  24.5 2.4 %copy-start.2 = (bf16[9,20,20]{2,1,0:T(8,128)(2,1)S(1)}, bf16[9,20,20]{2,1,0:T(8,128)(2,1)}, u32[]{:S(2)}) copy-start(bf16[9,20,20]{2,1,0:T(8,128)(2,1)} %param.9) | copy-start | bytes 21604
  24.5 11.4 %copy-start.3 = (s32[2]{0:T(128)S(1)}, s32[2]{0:T(128)}, u32[]{:S(2)}) copy-start(s32[2]{0:T(128)} %param.11) | copy-start | bytes 28
  24.5 11.5 %copy-start.4 = (bf16[9,2,3]{0,1,2:T(2,128)(2,1)S(1)}, bf16[9,2,3]{0,1,2:T(2,128)(2,1)}, u32[]{:S(2)}) copy-start(bf16[9,2,3]{0,1,2:T(2,128)(2,1)} %param.10) | copy-start | bytes 328
  27.5 10.5 %collective-permute-start = (bf16[2,9,20,384]{3,2,0,1:T(8,128)(2,1)S(1)}, bf16[2,9,20,384]{3,2,0,1:T(8,128)(2,1)S(1)}, u32[]{:S(2)}, u32[]{:S(2)}) collective-permute-start(bf16[2,9,20,384]{3,2,0,1:T(8,128)(2,1)S(1)} %fusion.4), channel_id=1, source_target_pairs={{0,32},{32,64},{64,96},{96,128},{128,160},{160,192},{192,224},{224... | collective-permute-start | bytes 829448 | tf_op jit(solution)/shard_map/ppermute | solution.py:17
  34.0 9.6 %collective-permute-start.1 = (bf16[2,9,20,384]{3,2,0,1:T(8,128)(2,1)S(1)}, bf16[2,9,20,384]{3,2,0,1:T(8,128)(2,1)S(1)}, u32[]{:S(2)}, u32[]{:S(2)}) collective-permute-start(bf16[2,9,20,384]{3,2,0,1:T(8,128)(2,1)S(1)} %fusion.4), channel_id=1, source_target_pairs={{32,0},{64,32},{96,64},{128,96},{160,128},{192,160},{224,192},{256... | collective-permute-start | bytes 829448 | tf_op jit(solution)/shard_map/ppermute | solution.py:20
  44.5 14.1 %copy-start.1 = (bf16[2,12,640]{2,0,1:T(2,128)(2,1)S(1)}, bf16[2,12,640]{2,0,1:T(2,128)(2,1)}, u32[]{:S(2)}) copy-start(bf16[2,12,640]{2,0,1:T(2,128)(2,1)} %param.7) | copy-start | bytes 92164

commit v2 on v0

v2 whole, which is shorter than its diff:
```python
import jax
import jax.numpy as jnp
from jax import lax
from jax.experimental import pallas as pl
from jax.experimental.pallas import tpu as pltpu
from jax.sharding import PartitionSpec as P

MESH = pl.DeviceIdType.MESH
F32 = jnp.float32
BF16 = jnp.bfloat16
X_CHIPS, Z_CHIPS = 4, 8
LANES = 128
SLOT = 32
AHEAD = 8


def peers():
    steps = [(dx, dz) for dx in range(X_CHIPS) for dz in range(Z_CHIPS) if dx or dz]
    return sorted(steps, key=lambda s: -(min(s[0], X_CHIPS - s[0]) + min(s[1], Z_CHIPS - s[1])))


def lane_index(rows=8):
    return lax.broadcasted_iota(jnp.int32, (rows, LANES), 1)


def erf_gelu(value):
    return 0.5 * value * (1.0 + lax.erf(value * 0.7071067811865476))


def kernel(
    latent_hbm, filter_hbm, mix_hbm, band_hbm, up_hbm, down_hbm, out_ref,
    latent_in, filter_in, mix_in, band_in, up_in, down_in,
    rows, parts_out, parts_own, parts_low, parts_high, back_out, back_in,
    gathered, stack, table, mix_wide, mixer, turned,
    load_sem, out_sem, own_sem, low_sem, high_sem, halo_sem, back_send_sem, back_sem,
):
    lat, lon = lax.axis_index("lat"), lax.axis_index("lon")
    lats, lons = lax.axis_size("lat"), lax.axis_size("lon")
    width = latent_in.shape[1]
    channels = latent_in.shape[2]
    group = mix_in.shape[2]
    count, length = filter_in.shape
    my_x, my_z = lon // Z_CHIPS, lon % Z_CHIPS
    others = [
        lax.rem(my_x + dx, X_CHIPS) * Z_CHIPS + lax.rem(my_z + dz, Z_CHIPS) for dx, dz in peers()
    ]
    has_low, has_high = lat > 0, lat < lats - 1

    barrier = pltpu.get_barrier_semaphore()
    for other in others:
        pl.semaphore_signal(barrier, inc=1, device_id=(lat, other), device_id_type=MESH)

    @pl.when(has_low)
    def _():
        pl.semaphore_signal(barrier, inc=1, device_id=(lat - 1, lon), device_id_type=MESH)

    @pl.when(has_high)
    def _():
        pl.semaphore_signal(barrier, inc=1, device_id=(lat + 1, lon), device_id_type=MESH)

    loads = [
        pltpu.make_async_copy(source, target, load_sem.at[n])
        for n, (source, target) in enumerate(
            (
                (latent_hbm, latent_in),
                (filter_hbm, filter_in),
                (mix_hbm, mix_in),
                (band_hbm, band_in),
                (up_hbm, up_in),
                (down_hbm, down_in),
            )
        )
    ]
    for load in loads:
        load.start()

    rows[...] = jnp.zeros(rows.shape, F32)
    loads[0].wait()
    for i in range(2):
        values = latent_in[i].astype(F32)
        rows[8 * i : 8 * i + 8, :] = values[0:AHEAD]
        rows[16 + 8 * i : 16 + 8 * i + width - AHEAD, :] = values[AHEAD:width]

    lane = lane_index()
    odd = lax.rem(lon, 2) == 1
    tiles = [rows[8 * q : 8 * q + 8, :] for q in range(4)]
    for q in (2, 3):
        tiles[q] = jnp.where(odd, pltpu.roll(tiles[q], 4, 0), tiles[q])
    for g in range(channels // group):
        tile, place = divmod(g * group, LANES)
        message = jnp.zeros((8, LANES), F32)
        for q in range(4):
            piece = tiles[q][:, tile * LANES : (tile + 1) * LANES]
            if place + group > LANES:
                after = tiles[q][:, (tile + 1) * LANES : (tile + 2) * LANES]
                piece = jnp.where(lane >= place, piece, after)
            shift = (SLOT * q - place) % LANES
            if shift:
                piece = pltpu.roll(piece, shift, 1)
            inside = (lane >= SLOT * q) & (lane < SLOT * q + group)
            message = jnp.where(inside, piece, message)
        parts_out[g] = message.astype(BF16)
    parts_own[lon] = parts_out[lon]

    pl.semaphore_wait(
        barrier, lons - 1 + has_low.astype(jnp.int32) + has_high.astype(jnp.int32)
    )

    def send(source, target, send_sem, recv_sem, device):
        return pltpu.make_async_remote_copy(
            src_ref=source,
            dst_ref=target,
            send_sem=send_sem,
            recv_sem=recv_sem,
            device_id=device,
            device_id_type=MESH,
        )

    for other in others:
        send(parts_out.at[other], parts_own.at[lon], out_sem, own_sem, (lat, other)).start()

    loads[1].wait()
    row16 = lax.broadcasted_iota(jnp.int32, (8, length), 0)
    filters = filter_in[...].astype(F32)
    for k in range(count):
        first = jnp.broadcast_to(filters[k : k + 1, :], (8, length))
        first = pltpu.roll(first, 0, 1, stride=1, stride_axis=0)
        last = jnp.where(row16 < 4, pltpu.roll(first, AHEAD, 1), pltpu.roll(first, 2 * AHEAD, 1))
        first = jnp.concatenate([first, pltpu.roll(first, width, 1)], axis=0)
        last = jnp.concatenate([last, pltpu.roll(last, 2 * width, 1)], axis=0)
        base = k * length
        for p in range(lons // 2):
            turn = pltpu.roll(first, 2 * width * p, 1) if p else first
            table[base + 16 * p : base + 16 * p + 16, :] = turn.astype(BF16)
        base += 8 * lons
        for p in range(lons // 4):
            turn = pltpu.roll(last, 4 * width * p, 1) if p else last
            table[base + 16 * p : base + 16 * p + 16, :] = turn.astype(BF16)

    loads[2].wait()
    loads[3].wait()
    mix_wide[...] = jnp.zeros(mix_wide.shape, F32)
    slot = lax.broadcasted_iota(jnp.int32, (1, LANES), 1) // SLOT
    for k in range(count):
        mix_wide[k, 0:group, 0:group] = mix_in[k].astype(F32)
        once = mix_wide[k]
        all_slots = once
        for q in range(1, 4):
            all_slots = all_slots + pltpu.roll(once, SLOT * q, 1)
        bands = band_in[k].astype(F32)
        band = [[bands[i : i + 1, t : t + 1] for t in range(3)] for i in range(2)]

        def lanes_of(values):
            scale = jnp.zeros((1, LANES), F32)
            for q, value in values:
                scale = jnp.where(slot == q, value, scale)
            return (all_slots * scale).astype(BF16)

        top, end = 2 * SLOT * k, 2 * SLOT * k + SLOT
        mixer[top : top + SLOT, 0:LANES] = lanes_of([(0, band[0][0]), (1, band[0][1]), (2, band[0][2])])
        mixer[top : top + SLOT, LANES:] = jnp.zeros((SLOT, LANES), BF16)
        mixer[end : end + SLOT, 0:LANES] = lanes_of([(3, band[1][0])])
        mixer[end : end + SLOT, LANES:] = lanes_of([(0, band[1][1]), (1, band[1][2])])

    turned[length:, :] = jnp.zeros((turned.shape[0] - length, LANES), F32)
    stack[6 * SLOT :, :] = jnp.zeros((2 * SLOT, length), BF16)

    others_count = lons - 1
    some = send(
        parts_out.at[pl.ds(0, others_count)], parts_own.at[pl.ds(0, others_count)], out_sem, own_sem, (lat, others[0])
    )
    some.wait_recv()
    to_low = send(parts_own, parts_high, halo_sem.at[0], high_sem, (lat - 1, lon))
    to_high = send(parts_own, parts_low, halo_sem.at[1], low_sem, (lat + 1, lon))

    @pl.when(has_low)
    def _():
        to_low.start()

    @pl.when(has_high)
    def _():
        to_high.start()

    def unfold(parts, row):
        for b in range(lons):
            gathered[8 * b : 8 * b + 8, :] = parts[b].astype(F32)
        half = gathered[...]
        first = half.T[0 : 2 * SLOT, :]
        pairs = half.reshape(lons // 2, 2, 8, LANES)
        last = (pairs[:, 0] + pairs[:, 1]).reshape(4 * lons, LANES).T[2 * SLOT : 4 * SLOT, :]
        stack[row : row + 2 * SLOT, 0 : 8 * lons] = first.astype(BF16)
        stack[row : row + 2 * SLOT, 8 * lons :] = last.astype(BF16)

    unfold(parts_own, 2 * SLOT)

    @pl.when(has_low)
    def _():
        to_high.wait_recv()
        unfold(parts_low, 0)

    @pl.when(jnp.logical_not(has_low))
    def _():
        stack[0 : 2 * SLOT, :] = jnp.zeros((2 * SLOT, length), BF16)

    @pl.when(has_high)
    def _():
        to_low.wait_recv()
        unfold(parts_high, 4 * SLOT)

    @pl.when(jnp.logical_not(has_high))
    def _():
        stack[4 * SLOT : 6 * SLOT, :] = jnp.zeros((2 * SLOT, length), BF16)

    mixed = jnp.dot(mixer[...], stack[...], preferred_element_type=F32).astype(BF16)
    side = jnp.concatenate([mixed[2 * SLOT * k : 2 * SLOT * (k + 1), :] for k in range(count)], axis=1)
    convolved = jnp.dot(side, table[...], preferred_element_type=F32)
    turned[0:length, :] = jnp.concatenate([convolved, convolved], axis=0).T

    for b in range(lons):
        start = turned[width * b : width * b + 8, :]
        rest = turned[width * b + AHEAD : width * b + AHEAD + 8, :]
        back_out[b] = jnp.where(lane < 2 * SLOT, start, rest).astype(BF16)
    back_in[lon] = back_out[lon]
    for other in others:
        send(back_out.at[other], back_in.at[lon], back_send_sem, back_sem, (lat, other)).start()

    loads[4].wait()
    loads[5].wait()
    last = send(
        back_out.at[pl.ds(0, others_count)], back_in.at[pl.ds(0, others_count)], back_send_sem, back_sem, (lat, others[0])
    )
    last.wait_recv()

    blocks = channels // LANES
    sums = [[jnp.zeros((8, LANES), F32) for _ in range(blocks)] for _ in range(4)]
    for g in range(channels // group):
        tile, place = divmod(g * group, LANES)
        message = back_in[g].astype(F32)
        for q in range(4):
            shift = (place - SLOT * q) % LANES
            piece = pltpu.roll(message, shift, 1) if shift else message
            inside = (lane >= place) & (lane < place + group)
            sums[q][tile] = jnp.where(inside, piece, sums[q][tile])
            if place + group > LANES:
                sums[q][tile + 1] = jnp.where(lane < place + group - LANES, piece, sums[q][tile + 1])
    turned_back = jnp.concatenate([jnp.concatenate(one, axis=1) for one in sums], axis=0)

    summed = (rows[...] + turned_back).astype(BF16).astype(F32)
    mean = jnp.mean(summed, axis=1, keepdims=True)
    centred = summed - mean
    var = jnp.mean(centred * centred, axis=1, keepdims=True)
    normed = (centred * lax.rsqrt(var + 1e-05)).astype(BF16)
    hidden = erf_gelu(jnp.dot(normed, up_in[...], preferred_element_type=F32)).astype(BF16)
    result = summed + jnp.dot(hidden, down_in[...], preferred_element_type=F32)
    result = result.astype(BF16)
    for i in range(2):
        out_ref[i, 0:AHEAD, :] = result[8 * i : 8 * i + 8]
        out_ref[i, AHEAD:width, :] = result[16 + 8 * i : 16 + 8 * i + width - AHEAD]

    some.wait_send()
    last.wait_send()

    @pl.when(has_low)
    def _():
        to_low.wait_send()

    @pl.when(has_high)
    def _():
        to_high.wait_send()


def local(latent, lon_filter, mix_weight, band_weight, offsets, w_up, w_down):
    del offsets
    count, length = lon_filter.shape
    lons = lax.axis_size("lon")
    channels, hidden = w_up.shape
    parts = pltpu.VMEM((lons, 8, LANES), BF16)
    whole = pl.BlockSpec(memory_space=pl.ANY)
    return pl.pallas_call(
        kernel,
        out_shape=jax.ShapeDtypeStruct(latent.shape, latent.dtype),
        in_specs=[whole] * 6,
        out_specs=pl.BlockSpec(memory_space=pltpu.VMEM),
        scratch_shapes=[
            pltpu.VMEM(latent.shape, BF16),
            pltpu.VMEM(lon_filter.shape, BF16),
            pltpu.VMEM(mix_weight.shape, BF16),
            pltpu.VMEM(band_weight.shape, BF16),
            pltpu.VMEM(w_up.shape, BF16),
            pltpu.VMEM(w_down.shape, BF16),
            pltpu.VMEM((4 * 8, channels), F32),
            parts,
            parts,
            parts,
            parts,
            parts,
            parts,
            pltpu.VMEM((8 * lons, LANES), F32),
            pltpu.VMEM((8 * SLOT, length), BF16),
            pltpu.VMEM((count * length, length), BF16),
            pltpu.VMEM((count, SLOT, LANES), F32),
            pltpu.VMEM((count * 2 * SLOT, 8 * SLOT), BF16),
            pltpu.VMEM((length + 8, LANES), F32),
            pltpu.SemaphoreType.DMA((6,)),
            pltpu.SemaphoreType.DMA,
            pltpu.SemaphoreType.DMA,
            pltpu.SemaphoreType.DMA,
            pltpu.SemaphoreType.DMA,
            pltpu.SemaphoreType.DMA((2,)),
            pltpu.SemaphoreType.DMA,
            pltpu.SemaphoreType.DMA,
        ],
        compiler_params=pltpu.CompilerParams(collective_id=0, has_side_effects=True),
    )(latent, lon_filter, mix_weight, band_weight, w_up, w_down)


def solution(mesh):
    return jax.shard_map(
        local,
        mesh=mesh,
        in_specs=(
            P("lat", "lon", None),
            P(),
            P(None, "lon", None),
            P(None, "lat", None),
            P("lat"),
            P(),
            P(),
        ),
        out_specs=P("lat", "lon", None),
        check_vma=False,
    )
```

time: 601 us -> 35.9 us (0.06)
  local copies, waits for them, and re-layouts: 547 us -> 4.16 us
  Pallas kernels: 0 us -> 31.4 us
  starting transfers between devices: 20.1 us -> 0 us
  blocking collectives: 18 us -> 0 us
  waiting for transfers between devices: 7.37 us -> 0 us
  matrix products: 6.72 us -> 0 us
    gather x2 -> x0, local copies, waits for them, and re-layouts: 540 us -> none  [circulant(): return lon_filter[:, index_table]]
    pallas_call x0 -> x1, Pallas kernels: none -> 31.4 us  [local(): pl.pallas_call(kernel, out_shape=jax.ShapeDtypeStruct(latent.shape, laten...]
    all_to_all x1 -> x0, blocking collectives: 18 us -> none  [local(): lax.all_to_all(convolved, 'lon', split_axis=2, concat_axis=1, tiled=True)]
    all_to_all x1 -> x0, starting transfers between devices: 12.9 us -> none  [local(): lax.all_to_all(latent, 'lon', split_axis=2, concat_axis=1, tiled=True)]
    ppermute x2 -> x0, waiting for transfers between devices: 7.37 us -> none  [the longest x1 5.61 us: extended(): lax.ppermute(lax.slice_in_dim(block, 0, width, axis=dim), axis, backward)]
    ppermute x2 -> x0, starting transfers between devices: 7.17 us -> none  [the longest x1 5.25 us: extended(): lax.ppermute(lax.slice_in_dim(block, block.shape[dim] - width, None, axis...]
    dot_general x5 -> x0, matrix products: 6.72 us -> none  [the longest x1 2.93 us: local(): lax.dot_general(grouped, lon_table, (((1,), (2,)), ((), ())), preferred_e...]
  transfers between devices with their start and end apart: 3 -> 0, of which waited for: 2 -> 0; matrix products, arithmetic and copies ran while one was open for 90% -> 0% of each run, Pallas kernels for 0% -> 0%
where the time goes in v2:
time: 35.9 us; the launch traced here: 35.6 us
  Pallas kernels  31.4 us (87%)
  local copies, waits for them, and re-layouts  4.16 us (12%)
    pallas_call x1, Pallas kernels, local(): pl.pallas_call(kernel, out_shape=jax.ShapeDtypeStruct(latent.shape, laten...  31.4 us
    unnamed x2, local copies, waits for them, and re-layouts  2.74 us
    pallas_call x1, local copies, waits for them, and re-layouts, local(): pl.pallas_call(kernel, out_shape=jax.ShapeDtypeStruct(latent.shape, laten...  1.41 us

profile of v2, /device:TPU:25, one launch (start us, length us, event | category | flops | bytes accessed | tf_op | source)
XLA Modules:
  0.0 35.6 jit_solution(9860392878600649425)
XLA Ops:
  0.0 1.4 %copy.8.band_hbm = bf16[9,2,3]{2,1,0:T(2,128)(2,1)} copy(bf16[9,2,3]{0,1,2:T(2,128)(2,1)} %param.10) | data formatting | bytes 216 | tf_op args[3]
  1.4 1.4 %copy.7.latent_hbm = bf16[2,12,640]{2,1,0:T(8,128)(2,1)} copy(bf16[2,12,640]{2,0,1:T(2,128)(2,1)} %param.7) | data formatting | bytes 61440 | tf_op args[0]
  2.7 31.4 %shard_map.64 = bf16[2,12,640]{2,1,0:T(8,128)(2,1)} custom-call(bf16[2,12,640]{2,1,0:T(8,128)(2,1)} %copy.7.latent_hbm, bf16[9,384]{1,0:T(8,128)(2,1)} %filter_hbm.1, bf16[9,20,20]{2,1,0:T(8,128)(2,1)} %mix_hbm.1, bf16[9,2,3]{2,1,0:T(2,128)(2,1)} %copy.8.band_hbm, bf16[640,1280]{1,0:T(8,128)(2,1)} %up_hbm.1, bf16[1280,640]{1,0:T(8,128)(2,1)} %down_hbm.1), custom_call_target="tpu_custom_call" | custom-call | tf_op jit(solution)/shard_map/pallas_call | solution.py:279
  34.2 1.4 %copy.9 = bf16[2,12,640]{2,0,1:T(2,128)(2,1)} copy(bf16[2,12,640]{2,1,0:T(8,128)(2,1)} %shard_map.64) | data formatting | bytes 61440 | tf_op jit(solution)/shard_map/pallas_call | solution.py:279

commit v3 on v0

v3 whole, which is shorter than its diff:
```python
import jax
import jax.numpy as jnp
from jax import lax
from jax.experimental import pallas as pl
from jax.experimental.pallas import tpu as pltpu
from jax.sharding import PartitionSpec as P

MESH = pl.DeviceIdType.MESH
F32 = jnp.float32
BF16 = jnp.bfloat16
X_CHIPS, Z_CHIPS = 4, 8
WORK_Z = (6, 7, 0, 1)
WORKERS = X_CHIPS * len(WORK_Z)
WORK_LON = [x * Z_CHIPS + z for x in range(X_CHIPS) for z in WORK_Z]
LANES = 128
AHEAD = 8


def erf_gelu(value):
    return 0.5 * value * (1.0 + lax.erf(value * 0.7071067811865476))


def kernel(
    latent_hbm, filter_hbm, mix_hbm, band_hbm, up_hbm, down_hbm, out_ref,
    latent_in, filter_in, mix_in, band_in, up_in, down_in,
    points, rows, parts_out, parts_in, back_out, back_in,
    gathered, ends, stack, table, mix_wide, mixer, turned, turned_last,
    load_sem, small_send_sem, mix_sem, band_sem, out_sem, side_sem, in_sem, back_send_sem, back_sem,
):
    lat, lon = lax.axis_index("lat"), lax.axis_index("lon")
    lats, lons = lax.axis_size("lat"), lax.axis_size("lon")
    width, _, channels = latent_in.shape
    count, length = filter_in.shape
    group = mix_in.shape[3]
    share = channels // WORKERS
    core = lax.rem(lat, 2)
    base = lat - core
    my_x, my_z = lon // Z_CHIPS, lax.rem(lon, Z_CHIPS)
    my_turn = lax.rem(my_z + Z_CHIPS - WORK_Z[0], Z_CHIPS)
    my_work = my_x * len(WORK_Z) + my_turn
    work_chip = my_turn < len(WORK_Z)
    works = work_chip & (core == 1)
    idle = jnp.logical_not(works)
    has_low, has_high = base > 0, base + 2 < lats
    aside = base + jnp.where(core == 0, -1, 3)
    has_side = jnp.where(core == 0, base > 0, base + 2 < lats)

    def load(source, target, n):
        return pltpu.make_async_copy(source, target, load_sem.at[n])

    latent_load = load(latent_hbm, latent_in, 0)
    filter_load = load(filter_hbm, filter_in, 1)
    band_load = load(band_hbm, band_in.at[1], 2)
    up_load = load(up_hbm, up_in, 3)
    down_load = load(down_hbm, down_in, 4)
    latent_load.start()

    def send(source, target, send_sem, recv_sem, device):
        return pltpu.make_async_remote_copy(
            src_ref=source,
            dst_ref=target,
            send_sem=send_sem,
            recv_sem=recv_sem,
            device_id=device,
            device_id_type=MESH,
        )

    barrier = pltpu.get_barrier_semaphore()

    def signal(to_lat, to_lon):
        pl.semaphore_signal(barrier, inc=1, device_id=(to_lat, to_lon), device_id_type=MESH)

    @pl.when(works)
    def _():
        for z in reversed(range(Z_CHIPS)):
            for x in range(X_CHIPS):
                signal(base, x * Z_CHIPS + z)

        @pl.when(has_high)
        def _():
            for z in reversed(range(Z_CHIPS)):
                for x in range(X_CHIPS):
                    signal(base + 2, x * Z_CHIPS + z)

        for n in range(1, lons):
            signal(base + 1, lax.rem(lon + n, lons))

        @pl.when(has_low)
        def _():
            for z in reversed(range(Z_CHIPS)):
                for x in range(X_CHIPS):
                    signal(base - 1, x * Z_CHIPS + z)

    filter_load.start()
    band_load.start()

    blocks = channels // LANES
    columns = [slice(LANES * t, LANES * (t + 1)) for t in range(blocks)]
    rest = width - AHEAD
    places = [
        (slice(0, AHEAD), pl.ds(0, AHEAD, stride=2)),
        (slice(AHEAD, 2 * AHEAD), pl.ds(1, AHEAD, stride=2)),
        (slice(2 * AHEAD, 2 * AHEAD + rest), pl.ds(2 * AHEAD, rest, stride=2)),
        (slice(2 * AHEAD + rest, 2 * width), pl.ds(2 * AHEAD + 1, rest, stride=2)),
    ]
    latent_load.wait()
    for t, column in enumerate(columns):
        for n in range(width):
            points[t, 2 * n : 2 * n + 2, :] = latent_in[n, :, column].astype(F32)
        for place, point in places:
            rows[place, column] = points[t, point, :]

    lane = lax.broadcasted_iota(jnp.int32, (8, LANES), 1)
    upper = lax.broadcasted_iota(jnp.int32, (8, LANES), 0) < rest
    tiles = [rows[8 * q : 8 * q + 8, :] for q in range(3)]
    tiles[2] = jnp.where(lax.rem(lon, 2) == 1, pltpu.roll(tiles[2], rest, 0), tiles[2])
    for w in range(WORKERS):
        tile, place = divmod(w * share, LANES)
        message = jnp.zeros((8, LANES), F32)
        for q in range(3):
            piece = tiles[q][:, columns[tile]]
            if place + share > LANES:
                piece = jnp.where(lane >= place, piece, tiles[q][:, columns[tile + 1]])
            shift = (share * q - place) % LANES
            if shift:
                piece = pltpu.roll(piece, shift, 1)
            inside = (lane >= share * q) & (lane < share * (q + 1))
            message = jnp.where(inside, piece, message)
        parts_out[w] = message.astype(BF16)

    @pl.when(works)
    def _():
        parts_in[2, lon] = parts_out[my_work]

    pl.semaphore_wait(
        barrier,
        WORKERS - works.astype(jnp.int32) + jnp.where(has_side, WORKERS, 0),
    )

    mix_work = lon // 2
    mix_lon = (mix_work // len(WORK_Z)) * Z_CHIPS + lax.rem(lax.rem(mix_work, len(WORK_Z)) + WORK_Z[0], Z_CHIPS)
    half = lax.rem(lon, 2)
    mix_send = send(mix_hbm, mix_in.at[half], small_send_sem, mix_sem.at[half], (lat, mix_lon))
    mix_copy = pltpu.make_async_copy(mix_hbm, mix_in.at[half], mix_sem.at[half])
    band_send = send(band_hbm, band_in.at[0], small_send_sem, band_sem, (base + 1, lon))
    mix_away = (core == 1) & (mix_lon != lon)
    band_away = (core == 0) & work_chip

    @pl.when(band_away)
    def _():
        band_send.start()

    @pl.when(mix_away)
    def _():
        mix_send.start()

    @pl.when((core == 1) & (mix_lon == lon))
    def _():
        mix_copy.start()

    @pl.when(has_side)
    def _():
        slot = jnp.where(core == 0, 3, 0)
        for w, to_lon in enumerate(WORK_LON):
            send(parts_out.at[w], parts_in.at[slot, lon], side_sem, in_sem.at[slot], (aside, to_lon)).start()

    for w, to_lon in enumerate(WORK_LON):

        @pl.when(jnp.logical_not(works & (my_work == w)))
        def _(w=w, to_lon=to_lon):
            send(parts_out.at[w], parts_in.at[core + 1, lon], out_sem, in_sem.at[core + 1], (base + 1, to_lon)).start()

    up_load.start()
    down_load.start()
    filter_load.wait()
    band_load.wait()

    @pl.when(works)
    def _():
        row8 = lax.broadcasted_iota(jnp.int32, (8, length), 0)
        filters = filter_in[...].astype(F32)
        for k in range(count):
            first = jnp.broadcast_to(filters[k : k + 1, :], (8, length))
            first = pltpu.roll(first, 0, 1, stride=1, stride_axis=0)
            last = jnp.where(row8 < rest, pltpu.roll(first, AHEAD, 1), pltpu.roll(first, 2 * AHEAD, 1))
            first = jnp.concatenate([first, pltpu.roll(first, width, 1)], axis=0)
            last = jnp.concatenate([last, pltpu.roll(last, 2 * width, 1)], axis=0)
            top = k * length
            for p in range(lons // 2):
                turn = pltpu.roll(first, 2 * width * p, 1) if p else first
                table[top + 16 * p : top + 16 * p + 16, :] = turn.astype(BF16)
            top += 8 * lons
            for p in range(lons // 4):
                turn = pltpu.roll(last, 4 * width * p, 1) if p else last
                table[top + 16 * p : top + 16 * p + 16, :] = turn.astype(BF16)

        mix_wide[...] = jnp.zeros(mix_wide.shape, F32)
        for h in range(2):
            send(mix_hbm, mix_in.at[h], small_send_sem, mix_sem.at[h], (lat, 0)).wait_recv()
        send(band_hbm, band_in.at[0], small_send_sem, band_sem, (base, lon)).wait_recv()
        third = lax.broadcasted_iota(jnp.int32, (1, LANES), 1) // share
        lower = lax.broadcasted_iota(jnp.int32, (share, LANES), 0) >= group
        bands = [band_in[o].astype(F32) for o in range(2)]
        empty = jnp.zeros((share, LANES), F32)
        for k in range(count):
            for h in range(2):
                mix_wide[group * h : group * (h + 1), 0:group] = mix_in[h, k].astype(F32)
            once = mix_wide[...]
            once = jnp.where(lower, pltpu.roll(once, group, 1), once)
            every = once + pltpu.roll(once, share, 1) + pltpu.roll(once, 2 * share, 1)
            for o in range(2):
                scaled = []
                for i in range(2):
                    scale = jnp.zeros((1, LANES), F32)
                    for t in range(3):
                        scale = jnp.where(third == t, bands[o][t, i : i + 1, k : k + 1], scale)
                    scaled.append(every * scale)
                whole = jnp.concatenate(
                    [
                        jnp.concatenate([scaled[0], empty], axis=1),
                        jnp.concatenate([empty, scaled[1]], axis=1),
                    ],
                    axis=0,
                )
                mixer[o, 2 * share * k : 2 * share * (k + 1), :] = whole.astype(BF16)

        turned[:, length:, :] = jnp.zeros((2, turned.shape[1] - length, LANES), F32)

        def unfold(n):
            for b in range(lons):
                gathered[8 * b : 8 * b + 8, :] = parts_in[n, b].astype(F32)
            for p in range(lons // 2):
                even, odd = gathered[16 * p : 16 * p + 8, :], gathered[16 * p + 8 : 16 * p + 16, :]
                one = pltpu.roll(jnp.where(upper, odd, even), rest, 0)
                one = pltpu.roll(one, LANES - 2 * share, 1)
                ends[8 * p : 8 * p + 8, :] = jnp.where(lane >= 2 * share, jnp.where(upper, even, odd), one)
            first, last = gathered[...].T, ends[...].T
            top = 2 * share * n
            stack[top : top + 2 * share, 0 : 8 * lons] = first[0 : 2 * share]
            stack[top : top + share, 8 * lons :] = last[2 * share : 3 * share]
            stack[top + share : top + 2 * share, 8 * lons :] = last[0:share]

        def arrive(n, members):
            taken = parts_in.at[n, pl.ds(0, members)]
            send(taken, taken, out_sem, in_sem.at[n], (lat, 0)).wait_recv()

        for n, there in ((0, has_low), (3, has_high)):

            @pl.when(there)
            def _(n=n):
                arrive(n, lons)
                unfold(n)

            @pl.when(jnp.logical_not(there))
            def _(n=n):
                stack[2 * share * n : 2 * share * (n + 1), :] = jnp.zeros((2 * share, length), F32)

        arrive(2, lons - 1)
        unfold(2)
        arrive(1, lons)
        unfold(1)

        pad = jnp.zeros((LANES - 3 * share, length), F32)
        sides = []
        for o in range(2):
            top = 2 * share * o
            wide = jnp.concatenate(
                [stack[top : top + 3 * share, :], pad, stack[top + 3 * share : top + 6 * share, :], pad], axis=0
            ).astype(BF16)
            mixed = jnp.dot(mixer[o], wide, preferred_element_type=F32).astype(BF16)
            sides.append(
                jnp.concatenate([mixed[2 * share * k : 2 * share * (k + 1), :] for k in range(count)], axis=1)
            )
        convolved = jnp.dot(jnp.concatenate(sides, axis=0), table[...], preferred_element_type=F32)

        for o in range(2):
            one = convolved[2 * share * o : 2 * share * (o + 1), :]
            one = jnp.concatenate([one, one[0:share], pad], axis=0).T
            turned[o, 0:length, :] = one
            turned_last[o] = pltpu.roll(one, share, 1)
        order = sorted(range(lons), key=lambda b: b % Z_CHIPS)
        for b in order:
            for o in (1, 0):
                start = turned[o, width * b : width * b + 8, :]
                end0 = turned[o, width * b + AHEAD : width * b + AHEAD + 8, :]
                end1 = turned_last[o, width * b + rest : width * b + rest + 8, :]
                message = jnp.where(lane < 2 * share, start, jnp.where(upper, end0, end1))
                back_out[o, b] = message.astype(BF16)
        back_in[my_work] = back_out[1, lon]
        for b in order:

            @pl.when(lon != b)
            def _(b=b):
                send(back_out.at[1, b], back_in.at[my_work], back_send_sem.at[1], back_sem, (base + 1, b)).start()

            send(back_out.at[0, b], back_in.at[my_work], back_send_sem.at[0], back_sem, (base, b)).start()

    def sent(buffer, members, sem):
        taken = buffer.at[pl.ds(0, members)]
        send(taken, taken, sem, back_sem, (lat, 0)).wait_send()

    def returned(members):
        taken = back_in.at[pl.ds(0, members)]
        send(taken, taken, out_sem, back_sem, (lat, 0)).wait_recv()

    up_load.wait()
    down_load.wait()

    @pl.when(works)
    def _():
        returned(WORKERS - 1)

    @pl.when(idle)
    def _():
        returned(WORKERS)

    sums = [[jnp.zeros((8, LANES), F32) for _ in range(blocks)] for _ in range(3)]
    for w in range(WORKERS):
        tile, place = divmod(w * share, LANES)
        message = back_in[w].astype(F32)
        for q in range(3):
            shift = (place - share * q) % LANES
            piece = pltpu.roll(message, shift, 1) if shift else message
            inside = (lane >= place) & (lane < place + share)
            sums[q][tile] = jnp.where(inside, piece, sums[q][tile])
            if place + share > LANES:
                sums[q][tile + 1] = jnp.where(lane < place + share - LANES, piece, sums[q][tile + 1])
    returned_rows = jnp.concatenate([jnp.concatenate(one, axis=1) for one in sums], axis=0)

    summed = (rows[...] + returned_rows).astype(BF16).astype(F32)
    mean = jnp.mean(summed, axis=1, keepdims=True)
    centred = summed - mean
    var = jnp.mean(centred * centred, axis=1, keepdims=True)
    normed = (centred * lax.rsqrt(var + 1e-05)).astype(BF16)
    hidden = erf_gelu(jnp.dot(normed, up_in[...], preferred_element_type=F32)).astype(BF16)
    result = summed + jnp.dot(hidden, down_in[...], preferred_element_type=F32)
    for t, column in enumerate(columns):
        for place, point in places:
            points[t, point, :] = result[place, column]
        for n in range(width):
            out_ref[n, :, column] = points[t, 2 * n : 2 * n + 2, :].astype(BF16)

    @pl.when(works)
    def _():
        sent(parts_out, WORKERS - 1, out_sem)
        sent(back_out.at[1], lons - 1, back_send_sem.at[1])
        sent(back_out.at[0], lons, back_send_sem.at[0])

    @pl.when(idle)
    def _():
        sent(parts_out, WORKERS, out_sem)

    @pl.when(has_side)
    def _():
        sent(parts_out, WORKERS, side_sem)

    @pl.when(mix_away)
    def _():
        mix_send.wait_send()

    @pl.when(band_away)
    def _():
        band_send.wait_send()


def local(latent, lon_filter, mix_weight, band_weight, offsets, w_up, w_down):
    del offsets
    latent, band_weight = jnp.transpose(latent, (1, 0, 2)), jnp.transpose(band_weight, (2, 1, 0))
    count, length = lon_filter.shape
    lons = lax.axis_size("lon")
    channels = w_up.shape[0]
    share = channels // WORKERS
    whole = pl.BlockSpec(memory_space=pl.ANY)
    result = pl.pallas_call(
        kernel,
        out_shape=jax.ShapeDtypeStruct(latent.shape, latent.dtype),
        in_specs=[whole] * 6,
        out_specs=pl.BlockSpec(memory_space=pltpu.VMEM),
        scratch_shapes=[
            pltpu.VMEM(latent.shape, BF16),
            pltpu.VMEM(lon_filter.shape, BF16),
            pltpu.VMEM((2, *mix_weight.shape), BF16),
            pltpu.VMEM((2, *band_weight.shape), BF16),
            pltpu.VMEM(w_up.shape, BF16),
            pltpu.VMEM(w_down.shape, BF16),
            pltpu.VMEM((channels // LANES, 2 * latent.shape[0], LANES), F32),
            pltpu.VMEM((2 * latent.shape[0], channels), F32),
            pltpu.VMEM((WORKERS, 8, LANES), BF16),
            pltpu.VMEM((4, lons, 8, LANES), BF16),
            pltpu.VMEM((2, lons, 8, LANES), BF16),
            pltpu.VMEM((WORKERS, 8, LANES), BF16),
            pltpu.VMEM((8 * lons, LANES), F32),
            pltpu.VMEM((4 * lons, LANES), F32),
            pltpu.VMEM((8 * share, length), F32),
            pltpu.VMEM((count * length, length), BF16),
            pltpu.VMEM((share, LANES), F32),
            pltpu.VMEM((2, count * 2 * share, 2 * LANES), BF16),
            pltpu.VMEM((2, length + 8, LANES), F32),
            pltpu.VMEM((2, length, LANES), F32),
            pltpu.SemaphoreType.DMA((5,)),
            pltpu.SemaphoreType.DMA,
            pltpu.SemaphoreType.DMA((2,)),
            pltpu.SemaphoreType.DMA,
            pltpu.SemaphoreType.DMA,
            pltpu.SemaphoreType.DMA,
            pltpu.SemaphoreType.DMA((4,)),
            pltpu.SemaphoreType.DMA((2,)),
            pltpu.SemaphoreType.DMA,
        ],
        compiler_params=pltpu.CompilerParams(collective_id=0, has_side_effects=True),
    )(latent, lon_filter, mix_weight, band_weight, w_up, w_down)
    return jnp.transpose(result, (1, 0, 2))


def solution(mesh):
    return jax.shard_map(
        local,
        mesh=mesh,
        in_specs=(
            P("lat", "lon", None),
            P(),
            P(None, "lon", None),
            P(None, "lat", None),
            P("lat"),
            P(),
            P(),
        ),
        out_specs=P("lat", "lon", None),
        check_vma=False,
    )
```

time: 601 us -> 31.7 us (0.05)
  local copies, waits for them, and re-layouts: 547 us -> 1.39 us
  Pallas kernels: 0 us -> 30.1 us
  starting transfers between devices: 20.1 us -> 0 us
  blocking collectives: 18 us -> 0 us
  waiting for transfers between devices: 7.37 us -> 0 us
  matrix products: 6.72 us -> 0 us
    gather x2 -> x0, local copies, waits for them, and re-layouts: 540 us -> none  [circulant(): return lon_filter[:, index_table]]
    pallas_call x0 -> x1, Pallas kernels: none -> 30.1 us  [local(): pl.pallas_call(kernel, out_shape=jax.ShapeDtypeStruct(latent.shape, laten...]
    all_to_all x1 -> x0, blocking collectives: 18 us -> none  [local(): lax.all_to_all(convolved, 'lon', split_axis=2, concat_axis=1, tiled=True)]
    all_to_all x1 -> x0, starting transfers between devices: 12.9 us -> none  [local(): lax.all_to_all(latent, 'lon', split_axis=2, concat_axis=1, tiled=True)]
    ppermute x2 -> x0, waiting for transfers between devices: 7.37 us -> none  [the longest x1 5.61 us: extended(): lax.ppermute(lax.slice_in_dim(block, 0, width, axis=dim), axis, backward)]
    ppermute x2 -> x0, starting transfers between devices: 7.17 us -> none  [the longest x1 5.25 us: extended(): lax.ppermute(lax.slice_in_dim(block, block.shape[dim] - width, None, axis...]
    dot_general x5 -> x0, matrix products: 6.72 us -> none  [the longest x1 2.93 us: local(): lax.dot_general(grouped, lon_table, (((1,), (2,)), ((), ())), preferred_e...]
  transfers between devices with their start and end apart: 3 -> 0, of which waited for: 2 -> 0; matrix products, arithmetic and copies ran while one was open for 90% -> 0% of each run, Pallas kernels for 0% -> 0%
where the time goes in v3:
time: 31.7 us; the launch traced here: 31.5 us
  Pallas kernels  30.1 us (95%)
  local copies, waits for them, and re-layouts  1.39 us (4%)
    pallas_call x1, Pallas kernels, local(): pl.pallas_call(kernel, out_shape=jax.ShapeDtypeStruct(latent.shape, laten...  30.1 us
    unnamed x1, local copies, waits for them, and re-layouts  1.39 us

profile of v3, /device:TPU:25, one launch (start us, length us, event | category | flops | bytes accessed | tf_op | source)
XLA Modules:
  0.0 31.5 jit_solution(6783613631148085398)
XLA Ops:
  0.0 30.1 %shard_map.64 = bf16[12,2,640]{2,1,0:T(2,128)(2,1)} custom-call(bf16[12,2,640]{2,1,0:T(2,128)(2,1)} %bitcast.4, bf16[9,384]{1,0:T(8,128)(2,1)} %filter_hbm.1, bf16[9,20,20]{2,1,0:T(8,128)(2,1)} %mix_hbm.1, bf16[3,2,9]{2,1,0:T(2,128)(2,1)} %bitcast.5, bf16[640,1280]{1,0:T(8,128)(2,1)} %up_hbm.1, bf16[1280,640]{1,0:T(8,128)(2,1)} %down_hbm.1), custom_call_target="tpu_custom_call" | custom-call | tf_op jit(solution)/shard_map/pallas_call | solution.py:374
  30.1 1.4 %copy.8 = bf16[2,12,640]{2,0,1:T(2,128)(2,1)} copy(bf16[2,12,640]{2,0,1:T(2,128)(2,1)} %bitcast.3) | data formatting | bytes 61440

commit v4 on v3

--- a/solution.py
+++ b/solution.py
@@ -9,9 +9,9 @@
 F32 = jnp.float32
 BF16 = jnp.bfloat16
 X_CHIPS, Z_CHIPS = 4, 8
-WORK_Z = (6, 7, 0, 1)
-WORKERS = X_CHIPS * len(WORK_Z)
-WORK_LON = [x * Z_CHIPS + z for x in range(X_CHIPS) for z in WORK_Z]
+WORK_Z = 2
+WORKERS = X_CHIPS * WORK_Z * 2
+WORK_AT = [(core, x * Z_CHIPS + z) for x in range(X_CHIPS) for z in range(WORK_Z) for core in range(2)]
 LANES = 128
 AHEAD = 8
 
@@ -36,13 +36,11 @@
     core = lax.rem(lat, 2)
     base = lat - core
     my_x, my_z = lon // Z_CHIPS, lax.rem(lon, Z_CHIPS)
-    my_turn = lax.rem(my_z + Z_CHIPS - WORK_Z[0], Z_CHIPS)
-    my_work = my_x * len(WORK_Z) + my_turn
-    work_chip = my_turn < len(WORK_Z)
-    works = work_chip & (core == 1)
+    my_work = (my_x * WORK_Z + my_z) * 2 + core
+    works = my_z < WORK_Z
     idle = jnp.logical_not(works)
     has_low, has_high = base > 0, base + 2 < lats
-    aside = base + jnp.where(core == 0, -1, 3)
+    aside = base + jnp.where(core == 0, -2, 2)
     has_side = jnp.where(core == 0, base > 0, base + 2 < lats)
 
     def load(source, target, n):
@@ -50,7 +48,7 @@
 
     latent_load = load(latent_hbm, latent_in, 0)
     filter_load = load(filter_hbm, filter_in, 1)
-    band_load = load(band_hbm, band_in.at[1], 2)
+    band_load = load(band_hbm, band_in.at[core], 2)
     up_load = load(up_hbm, up_in, 3)
     down_load = load(down_hbm, down_in, 4)
     latent_load.start()
@@ -74,7 +72,15 @@
     def _():
         for z in reversed(range(Z_CHIPS)):
             for x in range(X_CHIPS):
-                signal(base, x * Z_CHIPS + z)
+                to_lon = x * Z_CHIPS + z
+                for c in range(2):
+                    if z < WORK_Z:
+
+                        @pl.when((lon != to_lon) | (core != c))
+                        def _(c=c, to_lon=to_lon):
+                            signal(base + c, to_lon)
+                    else:
+                        signal(base + c, to_lon)
 
         @pl.when(has_high)
         def _():
@@ -82,9 +88,6 @@
                 for x in range(X_CHIPS):
                     signal(base + 2, x * Z_CHIPS + z)
 
-        for n in range(1, lons):
-            signal(base + 1, lax.rem(lon + n, lons))
-
         @pl.when(has_low)
         def _():
             for z in reversed(range(Z_CHIPS)):
@@ -93,6 +96,33 @@
 
     filter_load.start()
     band_load.start()
+
+    pl.semaphore_wait(
+        barrier,
+        WORKERS - works.astype(jnp.int32) + jnp.where(has_side, WORKERS, 0),
+    )
+
+    mix_work = lon // 2
+    mix_core = lax.rem(mix_work, 2)
+    mix_lon = (mix_work // (2 * WORK_Z)) * Z_CHIPS + lax.rem(mix_work // 2, WORK_Z)
+    half = lax.rem(lon, 2)
+    mix_send = send(mix_hbm, mix_in.at[half], small_send_sem.at[0], mix_sem.at[half], (base + mix_core, mix_lon))
+    mix_copy = pltpu.make_async_copy(mix_hbm, mix_in.at[half], mix_sem.at[half])
+    band_send = send(band_hbm, band_in.at[core], small_send_sem.at[1], band_sem, (base + 1 - core, lon))
+    mix_here = (core == mix_core) & (lon == mix_lon)
+    mix_away = (core == 1) & jnp.logical_not(mix_here)
+
+    @pl.when(works)
+    def _():
+        band_send.start()
+
+    @pl.when(mix_away)
+    def _():
+        mix_send.start()
+
+    @pl.when((core == 1) & mix_here)
+    def _():
+        mix_copy.start()
 
     blocks = channels // LANES
     columns = [slice(LANES * t, LANES * (t + 1)) for t in range(blocks)]
@@ -130,45 +160,19 @@
 
     @pl.when(works)
     def _():
-        parts_in[2, lon] = parts_out[my_work]
-
-    pl.semaphore_wait(
-        barrier,
-        WORKERS - works.astype(jnp.int32) + jnp.where(has_side, WORKERS, 0),
-    )
-
-    mix_work = lon // 2
-    mix_lon = (mix_work // len(WORK_Z)) * Z_CHIPS + lax.rem(lax.rem(mix_work, len(WORK_Z)) + WORK_Z[0], Z_CHIPS)
-    half = lax.rem(lon, 2)
-    mix_send = send(mix_hbm, mix_in.at[half], small_send_sem, mix_sem.at[half], (lat, mix_lon))
-    mix_copy = pltpu.make_async_copy(mix_hbm, mix_in.at[half], mix_sem.at[half])
-    band_send = send(band_hbm, band_in.at[0], small_send_sem, band_sem, (base + 1, lon))
-    mix_away = (core == 1) & (mix_lon != lon)
-    band_away = (core == 0) & work_chip
-
-    @pl.when(band_away)
-    def _():
-        band_send.start()
-
-    @pl.when(mix_away)
-    def _():
-        mix_send.start()
-
-    @pl.when((core == 1) & (mix_lon == lon))
-    def _():
-        mix_copy.start()
+        parts_in[core + 1, lon] = parts_out[my_work]
 
     @pl.when(has_side)
     def _():
         slot = jnp.where(core == 0, 3, 0)
-        for w, to_lon in enumerate(WORK_LON):
-            send(parts_out.at[w], parts_in.at[slot, lon], side_sem, in_sem.at[slot], (aside, to_lon)).start()
-
-    for w, to_lon in enumerate(WORK_LON):
-
-        @pl.when(jnp.logical_not(works & (my_work == w)))
-        def _(w=w, to_lon=to_lon):
-            send(parts_out.at[w], parts_in.at[core + 1, lon], out_sem, in_sem.at[core + 1], (base + 1, to_lon)).start()
+        for w, (c, to_lon) in enumerate(WORK_AT):
+            send(parts_out.at[w], parts_in.at[slot, lon], side_sem, in_sem.at[slot], (aside + c, to_lon)).start()
+
+    for w, (c, to_lon) in enumerate(WORK_AT):
+
+        @pl.when((lon != to_lon) | (core != c))
+        def _(w=w, c=c, to_lon=to_lon):
+            send(parts_out.at[w], parts_in.at[core + 1, lon], out_sem, in_sem.at[core + 1], (base + c, to_lon)).start()
 
     up_load.start()
     down_load.start()
@@ -196,8 +200,8 @@
 
         mix_wide[...] = jnp.zeros(mix_wide.shape, F32)
         for h in range(2):
-            send(mix_hbm, mix_in.at[h], small_send_sem, mix_sem.at[h], (lat, 0)).wait_recv()
-        send(band_hbm, band_in.at[0], small_send_sem, band_sem, (base, lon)).wait_recv()
+            send(mix_hbm, mix_in.at[h], small_send_sem.at[0], mix_sem.at[h], (base, lon)).wait_recv()
+        band_send.wait_recv()
         third = lax.broadcasted_iota(jnp.int32, (1, LANES), 1) // share
         lower = lax.broadcasted_iota(jnp.int32, (share, LANES), 0) >= group
         bands = [band_in[o].astype(F32) for o in range(2)]
@@ -255,10 +259,17 @@
             def _(n=n):
                 stack[2 * share * n : 2 * share * (n + 1), :] = jnp.zeros((2 * share, length), F32)
 
-        arrive(2, lons - 1)
-        unfold(2)
-        arrive(1, lons)
-        unfold(1)
+        for n in (1, 2):
+
+            @pl.when(core + 1 == n)
+            def _(n=n):
+                arrive(n, lons - 1)
+
+            @pl.when(core + 1 != n)
+            def _(n=n):
+                arrive(n, lons)
+
+            unfold(n)
 
         pad = jnp.zeros((LANES - 3 * share, length), F32)
         sides = []
@@ -286,14 +297,17 @@
                 end1 = turned_last[o, width * b + rest : width * b + rest + 8, :]
                 message = jnp.where(lane < 2 * share, start, jnp.where(upper, end0, end1))
                 back_out[o, b] = message.astype(BF16)
-        back_in[my_work] = back_out[1, lon]
+        back_in[my_work] = back_out[core, lon]
         for b in order:
-
-            @pl.when(lon != b)
-            def _(b=b):
-                send(back_out.at[1, b], back_in.at[my_work], back_send_sem.at[1], back_sem, (base + 1, b)).start()
-
-            send(back_out.at[0, b], back_in.at[my_work], back_send_sem.at[0], back_sem, (base, b)).start()
+            for o in (1, 0):
+                back = send(back_out.at[o, b], back_in.at[my_work], back_send_sem.at[o], back_sem, (base + o, b))
+                if b % Z_CHIPS < WORK_Z:
+
+                    @pl.when((lon != b) | (core != o))
+                    def _(back=back):
+                        back.start()
+                else:
+                    back.start()
 
     def sent(buffer, members, sem):
         taken = buffer.at[pl.ds(0, members)]
@@ -343,8 +357,17 @@
     @pl.when(works)
     def _():
         sent(parts_out, WORKERS - 1, out_sem)
-        sent(back_out.at[1], lons - 1, back_send_sem.at[1])
-        sent(back_out.at[0], lons, back_send_sem.at[0])
+        for o in range(2):
+
+            @pl.when(core == o)
+            def _(o=o):
+                sent(back_out.at[o], lons - 1, back_send_sem.at[o])
+
+            @pl.when(core != o)
+            def _(o=o):
+                sent(back_out.at[o], lons, back_send_sem.at[o])
+
+        band_send.wait_send()
 
     @pl.when(idle)
     def _():
@@ -357,10 +380,6 @@
     @pl.when(mix_away)
     def _():
         mix_send.wait_send()
-
-    @pl.when(band_away)
-    def _():
-        band_send.wait_send()
 
 
 def local(latent, lon_filter, mix_weight, band_weight, offsets, w_up, w_down):
@@ -398,7 +417,7 @@
             pltpu.VMEM((2, length + 8, LANES), F32),
             pltpu.VMEM((2, length, LANES), F32),
             pltpu.SemaphoreType.DMA((5,)),
-            pltpu.SemaphoreType.DMA,
+            pltpu.SemaphoreType.DMA((2,)),
             pltpu.SemaphoreType.DMA((2,)),
             pltpu.SemaphoreType.DMA,
             pltpu.SemaphoreType.DMA,

time: 31.7 us -> 27.6 us (0.87)
  Pallas kernels: 30.1 us -> 25.9 us
    pallas_call x1, Pallas kernels: 30.1 us -> 25.9 us  [local(): pl.pallas_call(kernel, out_shape=jax.ShapeDtypeStruct(latent.shape, laten...]
where the time goes in v4:
time: 27.6 us; the launch traced here: 27.3 us
  Pallas kernels  25.9 us (94%)
  local copies, waits for them, and re-layouts  1.39 us (5%)
    pallas_call x1, Pallas kernels, local(): pl.pallas_call(kernel, out_shape=jax.ShapeDtypeStruct(latent.shape, laten...  25.9 us
    unnamed x1, local copies, waits for them, and re-layouts  1.39 us

profile of v4, /device:TPU:25, one launch (start us, length us, event | category | flops | bytes accessed | tf_op | source)
XLA Modules:
  0.0 27.3 jit_solution(5078662440897956085)
XLA Ops:
  0.0 25.9 %shard_map.64 = bf16[12,2,640]{2,1,0:T(2,128)(2,1)} custom-call(bf16[12,2,640]{2,1,0:T(2,128)(2,1)} %bitcast.4, bf16[9,384]{1,0:T(8,128)(2,1)} %filter_hbm.1, bf16[9,20,20]{2,1,0:T(8,128)(2,1)} %mix_hbm.1, bf16[3,2,9]{2,1,0:T(2,128)(2,1)} %bitcast.5, bf16[640,1280]{1,0:T(8,128)(2,1)} %up_hbm.1, bf16[1280,640]{1,0:T(8,128)(2,1)} %down_hbm.1), custom_call_target="tpu_custom_call" | custom-call | tf_op jit(solution)/shard_map/pallas_call | solution.py:393
  25.9 1.4 %copy.8 = bf16[2,12,640]{2,0,1:T(2,128)(2,1)} copy(bf16[2,12,640]{2,0,1:T(2,128)(2,1)} %bitcast.3) | data formatting | bytes 61440

commit v5 on v4

--- a/solution.py
+++ b/solution.py
@@ -389,7 +389,7 @@
     lons = lax.axis_size("lon")
     channels = w_up.shape[0]
     share = channels // WORKERS
-    whole = pl.BlockSpec(memory_space=pl.ANY)
+    whole = pl.BlockSpec(memory_space=pltpu.HBM)
     result = pl.pallas_call(
         kernel,
         out_shape=jax.ShapeDtypeStruct(latent.shape, latent.dtype),
@@ -426,8 +426,8 @@
             pltpu.SemaphoreType.DMA((2,)),
             pltpu.SemaphoreType.DMA,
         ],
-        compiler_params=pltpu.CompilerParams(collective_id=0, has_side_effects=True),
-    )(latent, lon_filter, mix_weight, band_weight, w_up, w_down)
+        compiler_params=pltpu.CompilerParams(vmem_limit_bytes=16384 << 10, collective_id=0, has_side_effects=True),
+    )(*(pltpu.with_memory_space_constraint(x, pltpu.HBM) for x in (latent, lon_filter, mix_weight, band_weight, w_up, w_down)))
     return jnp.transpose(result, (1, 0, 2))
 
 

time: 27.6 us -> 26.2 us (0.949)
  local copies, waits for them, and re-layouts: 1.39 us -> 0.61 us
  Pallas kernels: 25.9 us -> 25.3 us
    unnamed x1, local copies, waits for them, and re-layouts: 1.39 us -> 0.61 us
    pallas_call x1, Pallas kernels: 25.9 us -> 25.3 us  [local(): pl.pallas_call(kernel, out_shape=jax.ShapeDtypeStruct(latent.shape, laten...]
where the time goes in v5:
time: 26.2 us; the launch traced here: 25.9 us
  Pallas kernels  25.3 us (97%)
  local copies, waits for them, and re-layouts  0.61 us (2%)
    pallas_call x1, Pallas kernels, local(): pl.pallas_call(kernel, out_shape=jax.ShapeDtypeStruct(latent.shape, laten...  25.3 us
    unnamed x1, local copies, waits for them, and re-layouts  0.61 us

profile of v5, /device:TPU:25, one launch (start us, length us, event | category | flops | bytes accessed | tf_op | source)
XLA Modules:
  0.0 25.9 jit_solution(9320026554696404810)
XLA Ops:
  0.0 25.3 %shard_map.64 = bf16[12,2,640]{2,1,0:T(2,128)(2,1)S(1)} custom-call(bf16[12,2,640]{2,1,0:T(2,128)(2,1)} %bitcast.4, bf16[9,384]{1,0:T(8,128)(2,1)} %filter_hbm.1, bf16[9,20,20]{2,1,0:T(8,128)(2,1)} %mix_hbm.1, bf16[3,2,9]{2,1,0:T(2,128)(2,1)} %bitcast.5, bf16[640,1280]{1,0:T(8,128)(2,1)} %up_hbm.1, bf16[1280,640]{1,0:T(8,128)(2,1)} %down_hbm.1), custom_call_target="tpu_custom_call" | custom-call | tf_op jit(solution)/shard_map/pallas_call | solution.py:393
  25.3 0.6 %copy.8 = bf16[2,12,640]{2,0,1:T(2,128)(2,1)} copy(bf16[2,12,640]{2,0,1:T(2,128)(2,1)S(1)} %bitcast.3) | data formatting | bytes 61440

commit v6 on v5

--- a/solution.py
+++ b/solution.py
@@ -14,6 +14,9 @@
 WORK_AT = [(core, x * Z_CHIPS + z) for x in range(X_CHIPS) for z in range(WORK_Z) for core in range(2)]
 LANES = 128
 AHEAD = 8
+GROUPS = 2
+WIDE = 2 * LANES
+PACK, PACK_ROWS = 6, 32
 
 
 def erf_gelu(value):
@@ -23,19 +26,22 @@
 def kernel(
     latent_hbm, filter_hbm, mix_hbm, band_hbm, up_hbm, down_hbm, out_ref,
     latent_in, filter_in, mix_in, band_in, up_in, down_in,
-    points, rows, parts_out, parts_in, back_out, back_in,
-    gathered, ends, stack, table, mix_wide, mixer, turned, turned_last,
+    points, rows, mix_own, mix_out, parts_out, parts_in, back_out, back_in,
+    gathered, stack, plain, table, mix_wide, mixer, total, turned, turned_last,
     load_sem, small_send_sem, mix_sem, band_sem, out_sem, side_sem, in_sem, back_send_sem, back_sem,
 ):
     lat, lon = lax.axis_index("lat"), lax.axis_index("lon")
     lats, lons = lax.axis_size("lat"), lax.axis_size("lon")
     width, _, channels = latent_in.shape
     count, length = filter_in.shape
-    group = mix_in.shape[3]
+    group = mix_own.shape[1]
+    members = lons // GROUPS
+    my_x, my_z = lon // Z_CHIPS, lax.rem(lon, Z_CHIPS)
+    my_place = my_z * X_CHIPS + my_x
+    my_group = my_place // members
     share = channels // WORKERS
     core = lax.rem(lat, 2)
     base = lat - core
-    my_x, my_z = lon // Z_CHIPS, lax.rem(lon, Z_CHIPS)
     my_work = (my_x * WORK_Z + my_z) * 2 + core
     works = my_z < WORK_Z
     idle = jnp.logical_not(works)
@@ -51,7 +57,13 @@
     band_load = load(band_hbm, band_in.at[core], 2)
     up_load = load(up_hbm, up_in, 3)
     down_load = load(down_hbm, down_in, 4)
+    mix_load = load(mix_hbm, mix_own, 5)
     latent_load.start()
+
+    @pl.when(core == 1)
+    def _():
+        mix_load.start()
+
 
     def send(source, target, send_sem, recv_sem, device):
         return pltpu.make_async_remote_copy(
@@ -106,8 +118,8 @@
     mix_core = lax.rem(mix_work, 2)
     mix_lon = (mix_work // (2 * WORK_Z)) * Z_CHIPS + lax.rem(mix_work // 2, WORK_Z)
     half = lax.rem(lon, 2)
-    mix_send = send(mix_hbm, mix_in.at[half], small_send_sem.at[0], mix_sem.at[half], (base + mix_core, mix_lon))
-    mix_copy = pltpu.make_async_copy(mix_hbm, mix_in.at[half], mix_sem.at[half])
+    mix_send = send(mix_out, mix_in.at[half], small_send_sem.at[0], mix_sem.at[half], (base + mix_core, mix_lon))
+    mix_copy = pltpu.make_async_copy(mix_out, mix_in.at[half], mix_sem.at[half])
     band_send = send(band_hbm, band_in.at[core], small_send_sem.at[1], band_sem, (base + 1 - core, lon))
     mix_here = (core == mix_core) & (lon == mix_lon)
     mix_away = (core == 1) & jnp.logical_not(mix_here)
@@ -115,14 +127,6 @@
     @pl.when(works)
     def _():
         band_send.start()
-
-    @pl.when(mix_away)
-    def _():
-        mix_send.start()
-
-    @pl.when((core == 1) & mix_here)
-    def _():
-        mix_copy.start()
 
     blocks = channels // LANES
     columns = [slice(LANES * t, LANES * (t + 1)) for t in range(blocks)]
@@ -143,7 +147,7 @@
     lane = lax.broadcasted_iota(jnp.int32, (8, LANES), 1)
     upper = lax.broadcasted_iota(jnp.int32, (8, LANES), 0) < rest
     tiles = [rows[8 * q : 8 * q + 8, :] for q in range(3)]
-    tiles[2] = jnp.where(lax.rem(lon, 2) == 1, pltpu.roll(tiles[2], rest, 0), tiles[2])
+    tiles[2] = jnp.where(lax.rem(my_x, 2) == 1, pltpu.roll(tiles[2], rest, 0), tiles[2])
     for w in range(WORKERS):
         tile, place = divmod(w * share, LANES)
         message = jnp.zeros((8, LANES), F32)
@@ -160,19 +164,40 @@
 
     @pl.when(works)
     def _():
-        parts_in[core + 1, lon] = parts_out[my_work]
+        parts_in[core + 1, my_place] = parts_out[my_work]
 
     @pl.when(has_side)
     def _():
         slot = jnp.where(core == 0, 3, 0)
         for w, (c, to_lon) in enumerate(WORK_AT):
-            send(parts_out.at[w], parts_in.at[slot, lon], side_sem, in_sem.at[slot], (aside + c, to_lon)).start()
+            send(parts_out.at[w], parts_in.at[slot, my_place], side_sem, in_sem.at[slot, my_group], (aside + c, to_lon)).start()
+
+    @pl.when(core == 1)
+    def _():
+        mix_load.wait()
+        mix_wide[...] = jnp.zeros(mix_wide.shape, F32)
+        for first in range(0, count, PACK):
+            packed = jnp.zeros((share, LANES), F32)
+            for n in range(min(PACK, count - first)):
+                mix_wide[0:group, 0:group] = mix_own[first + n].astype(F32)
+                packed = packed + (pltpu.roll(mix_wide[...], group * n, 1) if n else mix_wide[...])
+            mix_out[first // PACK] = packed[0:PACK_ROWS].astype(BF16)
+
+    @pl.when(mix_away)
+    def _():
+        mix_send.start()
+
+    @pl.when((core == 1) & mix_here)
+    def _():
+        mix_copy.start()
 
     for w, (c, to_lon) in enumerate(WORK_AT):
 
         @pl.when((lon != to_lon) | (core != c))
         def _(w=w, c=c, to_lon=to_lon):
-            send(parts_out.at[w], parts_in.at[core + 1, lon], out_sem, in_sem.at[core + 1], (base + c, to_lon)).start()
+            send(
+                parts_out.at[w], parts_in.at[core + 1, my_place], out_sem, in_sem.at[core + 1, my_group], (base + c, to_lon)
+            ).start()
 
     up_load.start()
     down_load.start()
@@ -182,35 +207,121 @@
     @pl.when(works)
     def _():
         row8 = lax.broadcasted_iota(jnp.int32, (8, length), 0)
+        column_of = lax.broadcasted_iota(jnp.int32, (length, length), 1)
+        chip_z, chip_x = column_of // (X_CHIPS * width), lax.rem(column_of // width, X_CHIPS)
+        column_of = (chip_x * Z_CHIPS + chip_z) * width + lax.rem(column_of, width)
+        order = (column_of == lax.broadcasted_iota(jnp.int32, (length, length), 0)).astype(F32).astype(BF16)
+        for g in range(GROUPS):
+            plain[WIDE * g + 12 * members : WIDE * (g + 1), :] = jnp.zeros((WIDE - 12 * members, length), BF16)
         filters = filter_in[...].astype(F32)
         for k in range(count):
             first = jnp.broadcast_to(filters[k : k + 1, :], (8, length))
             first = pltpu.roll(first, 0, 1, stride=1, stride_axis=0)
-            last = jnp.where(row8 < rest, pltpu.roll(first, AHEAD, 1), pltpu.roll(first, 2 * AHEAD, 1))
-            first = jnp.concatenate([first, pltpu.roll(first, width, 1)], axis=0)
-            last = jnp.concatenate([last, pltpu.roll(last, 2 * width, 1)], axis=0)
-            top = k * length
-            for p in range(lons // 2):
-                turn = pltpu.roll(first, 2 * width * p, 1) if p else first
-                table[top + 16 * p : top + 16 * p + 16, :] = turn.astype(BF16)
-            top += 8 * lons
-            for p in range(lons // 4):
-                turn = pltpu.roll(last, 4 * width * p, 1) if p else last
-                table[top + 16 * p : top + 16 * p + 16, :] = turn.astype(BF16)
-
-        mix_wide[...] = jnp.zeros(mix_wide.shape, F32)
+            step = Z_CHIPS * width
+            last = jnp.where(row8 < rest, pltpu.roll(first, AHEAD, 1), pltpu.roll(first, AHEAD + step - rest, 1))
+            first = jnp.concatenate([first, pltpu.roll(first, step, 1)], axis=0)
+            last = jnp.concatenate([last, pltpu.roll(last, 2 * step, 1)], axis=0)
+            for z in range(Z_CHIPS):
+                g, at = divmod(z * X_CHIPS, members)
+                for x in range(0, X_CHIPS, 2):
+                    shift = (x * step + z * width) % length
+                    turn = pltpu.roll(first, shift, 1) if shift else first
+                    row = WIDE * g + 8 * (at + x)
+                    plain[row : row + 16, :] = turn.astype(BF16)
+                turn = pltpu.roll(last, z * width, 1) if z else last
+                row = WIDE * g + 8 * members + 4 * at
+                plain[row : row + 16, :] = turn.astype(BF16)
+            for g in range(GROUPS):
+                top = (g * count + k) * WIDE
+                table[top : top + WIDE, :] = jnp.dot(
+                    plain[WIDE * g : WIDE * (g + 1), :], order, preferred_element_type=F32
+                ).astype(BF16)
+
+        gathered[:, 12 * members :, :] = jnp.zeros((4, WIDE - 12 * members, LANES), F32)
+
+        @pl.when(jnp.logical_not(has_low))
+        def _():
+            parts_in[0] = jnp.zeros(parts_in.shape[1:], BF16)
+
+        @pl.when(jnp.logical_not(has_high))
+        def _():
+            parts_in[3] = jnp.zeros(parts_in.shape[1:], BF16)
+
+        def arrive(n, g, some):
+            taken = parts_in.at[n, pl.ds(0, some)]
+            send(taken, taken, out_sem, in_sem.at[n, g], (base, lon)).wait_recv()
+
+        def unfold(n, g):
+            for p in range(members // 2):
+                even, odd = (parts_in[n, g * members + 2 * p + m].astype(F32) for m in range(2))
+                gathered[n, 16 * p : 16 * p + 8, :] = even
+                gathered[n, 16 * p + 8 : 16 * p + 16, :] = odd
+                one = pltpu.roll(jnp.where(upper, odd, even), rest, 0)
+                one = pltpu.roll(one, LANES - share, 1)
+                zero = pltpu.roll(jnp.where(upper, even, odd), LANES - 2 * share, 1)
+                row = 8 * members + 8 * p
+                gathered[n, row : row + 8, :] = jnp.where(lane < share, zero, one)
+            stack[2 * share * n : 2 * share * (n + 1), WIDE * g : WIDE * (g + 1)] = gathered[n].T[0 : 2 * share]
+
+        def take(g):
+            for n, there in ((0, has_low), (3, has_high)):
+
+                @pl.when(there)
+                def _(n=n):
+                    arrive(n, g, members)
+
+            for n in (1, 2):
+                if g * members < WORK_Z * X_CHIPS:
+                    own = (core + 1 == n) & (my_group == g)
+
+                    @pl.when(own)
+                    def _(n=n):
+                        arrive(n, g, members - 1)
+
+                    @pl.when(jnp.logical_not(own))
+                    def _(n=n):
+                        arrive(n, g, members)
+                else:
+                    arrive(n, g, members)
+            for n in range(4):
+                unfold(n, g)
+
+        def mix(g):
+            pad = jnp.zeros((LANES - 3 * share, WIDE), F32)
+            lanes = slice(WIDE * g, WIDE * (g + 1))
+            sides = []
+            for o in range(2):
+                top = 2 * share * o
+                wide = jnp.concatenate(
+                    [stack[top : top + 3 * share, lanes], pad, stack[top + 3 * share : top + 6 * share, lanes], pad],
+                    axis=0,
+                ).astype(BF16)
+                mixed = jnp.dot(mixer[o], wide, preferred_element_type=F32).astype(BF16)
+                sides.append(
+                    jnp.concatenate([mixed[2 * share * k : 2 * share * (k + 1), :] for k in range(count)], axis=1)
+                )
+            return jnp.concatenate(sides, axis=0)
+
+        def part(g, start, end):
+            return table[count * WIDE * g : count * WIDE * (g + 1), start:end]
+
+        take(0)
+
         for h in range(2):
-            send(mix_hbm, mix_in.at[h], small_send_sem.at[0], mix_sem.at[h], (base, lon)).wait_recv()
+            send(mix_out, mix_in.at[h], small_send_sem.at[0], mix_sem.at[h], (base, lon)).wait_recv()
         band_send.wait_recv()
         third = lax.broadcasted_iota(jnp.int32, (1, LANES), 1) // share
-        lower = lax.broadcasted_iota(jnp.int32, (share, LANES), 0) >= group
+        wide_lane = lax.broadcasted_iota(jnp.int32, (PACK_ROWS, LANES), 1)
         bands = [band_in[o].astype(F32) for o in range(2)]
         empty = jnp.zeros((share, LANES), F32)
         for k in range(count):
             for h in range(2):
-                mix_wide[group * h : group * (h + 1), 0:group] = mix_in[h, k].astype(F32)
+                shift = (group * h - group * (k % PACK)) % LANES
+                once = mix_in[h, k // PACK].astype(F32)
+                once = pltpu.roll(once, shift, 1) if shift else once
+                once = jnp.where((wide_lane >= group * h) & (wide_lane < group * (h + 1)), once, 0.0)
+                mix_wide[group * h : group * (h + 1), :] = once[0:group]
             once = mix_wide[...]
-            once = jnp.where(lower, pltpu.roll(once, group, 1), once)
             every = once + pltpu.roll(once, share, 1) + pltpu.roll(once, 2 * share, 1)
             for o in range(2):
                 scaled = []
@@ -228,86 +339,44 @@
                 )
                 mixer[o, 2 * share * k : 2 * share * (k + 1), :] = whole.astype(BF16)
 
+        total[...] = jnp.dot(mix(0), part(0, 0, length), preferred_element_type=F32)
         turned[:, length:, :] = jnp.zeros((2, turned.shape[1] - length, LANES), F32)
-
-        def unfold(n):
-            for b in range(lons):
-                gathered[8 * b : 8 * b + 8, :] = parts_in[n, b].astype(F32)
-            for p in range(lons // 2):
-                even, odd = gathered[16 * p : 16 * p + 8, :], gathered[16 * p + 8 : 16 * p + 16, :]
-                one = pltpu.roll(jnp.where(upper, odd, even), rest, 0)
-                one = pltpu.roll(one, LANES - 2 * share, 1)
-                ends[8 * p : 8 * p + 8, :] = jnp.where(lane >= 2 * share, jnp.where(upper, even, odd), one)
-            first, last = gathered[...].T, ends[...].T
-            top = 2 * share * n
-            stack[top : top + 2 * share, 0 : 8 * lons] = first[0 : 2 * share]
-            stack[top : top + share, 8 * lons :] = last[2 * share : 3 * share]
-            stack[top + share : top + 2 * share, 8 * lons :] = last[0:share]
-
-        def arrive(n, members):
-            taken = parts_in.at[n, pl.ds(0, members)]
-            send(taken, taken, out_sem, in_sem.at[n], (lat, 0)).wait_recv()
-
-        for n, there in ((0, has_low), (3, has_high)):
-
-            @pl.when(there)
-            def _(n=n):
-                arrive(n, lons)
-                unfold(n)
-
-            @pl.when(jnp.logical_not(there))
-            def _(n=n):
-                stack[2 * share * n : 2 * share * (n + 1), :] = jnp.zeros((2 * share, length), F32)
-
-        for n in (1, 2):
-
-            @pl.when(core + 1 == n)
-            def _(n=n):
-                arrive(n, lons - 1)
-
-            @pl.when(core + 1 != n)
-            def _(n=n):
-                arrive(n, lons)
-
-            unfold(n)
-
-        pad = jnp.zeros((LANES - 3 * share, length), F32)
-        sides = []
-        for o in range(2):
-            top = 2 * share * o
-            wide = jnp.concatenate(
-                [stack[top : top + 3 * share, :], pad, stack[top + 3 * share : top + 6 * share, :], pad], axis=0
-            ).astype(BF16)
-            mixed = jnp.dot(mixer[o], wide, preferred_element_type=F32).astype(BF16)
-            sides.append(
-                jnp.concatenate([mixed[2 * share * k : 2 * share * (k + 1), :] for k in range(count)], axis=1)
-            )
-        convolved = jnp.dot(jnp.concatenate(sides, axis=0), table[...], preferred_element_type=F32)
-
-        for o in range(2):
-            one = convolved[2 * share * o : 2 * share * (o + 1), :]
-            one = jnp.concatenate([one, one[0:share], pad], axis=0).T
-            turned[o, 0:length, :] = one
-            turned_last[o] = pltpu.roll(one, share, 1)
-        order = sorted(range(lons), key=lambda b: b % Z_CHIPS)
-        for b in order:
-            for o in (1, 0):
-                start = turned[o, width * b : width * b + 8, :]
-                end0 = turned[o, width * b + AHEAD : width * b + AHEAD + 8, :]
-                end1 = turned_last[o, width * b + rest : width * b + rest + 8, :]
-                message = jnp.where(lane < 2 * share, start, jnp.where(upper, end0, end1))
-                back_out[o, b] = message.astype(BF16)
+        take(1)
+        late = mix(1)
+
+        def finish(start, end, chips):
+            convolved = total[:, start:end] + jnp.dot(late, part(1, start, end), preferred_element_type=F32)
+            fill = jnp.zeros((LANES - 3 * share, end - start), F32)
+            for o in range(2):
+                one = convolved[2 * share * o : 2 * share * (o + 1), :]
+                one = jnp.concatenate([one, one[0:share], fill], axis=0).T
+                turned[o, start:end, :] = one
+                turned_last[o, start:end, :] = pltpu.roll(one, share, 1)
+            for z in chips:
+                for x in range(X_CHIPS):
+                    b, at = x * Z_CHIPS + z, (z * X_CHIPS + x) * width
+                    for o in range(2):
+                        begin = turned[o, at : at + 8, :]
+                        end0 = turned[o, at + AHEAD : at + AHEAD + 8, :]
+                        end1 = turned_last[o, at + rest : at + rest + 8, :]
+                        message = jnp.where(lane < 2 * share, begin, jnp.where(upper, end0, end1))
+                        back_out[o, b] = message.astype(BF16)
+            for z in chips:
+                for x in range(X_CHIPS):
+                    b = x * Z_CHIPS + z
+                    for o in range(2):
+                        back = send(back_out.at[o, b], back_in.at[my_work], back_send_sem.at[o], back_sem, (base + o, b))
+                        if z < WORK_Z:
+
+                            @pl.when((lon != b) | (core != o))
+                            def _(back=back):
+                                back.start()
+                        else:
+                            back.start()
+
+        finish(0, LANES, range(WORK_Z))
         back_in[my_work] = back_out[core, lon]
-        for b in order:
-            for o in (1, 0):
-                back = send(back_out.at[o, b], back_in.at[my_work], back_send_sem.at[o], back_sem, (base + o, b))
-                if b % Z_CHIPS < WORK_Z:
-
-                    @pl.when((lon != b) | (core != o))
-                    def _(back=back):
-                        back.start()
-                else:
-                    back.start()
+        finish(LANES, length, range(WORK_Z, Z_CHIPS))
 
     def sent(buffer, members, sem):
         taken = buffer.at[pl.ds(0, members)]
@@ -398,31 +467,34 @@
         scratch_shapes=[
             pltpu.VMEM(latent.shape, BF16),
             pltpu.VMEM(lon_filter.shape, BF16),
-            pltpu.VMEM((2, *mix_weight.shape), BF16),
+            pltpu.VMEM((2, pl.cdiv(count, PACK), PACK_ROWS, LANES), BF16),
             pltpu.VMEM((2, *band_weight.shape), BF16),
             pltpu.VMEM(w_up.shape, BF16),
             pltpu.VMEM(w_down.shape, BF16),
             pltpu.VMEM((channels // LANES, 2 * latent.shape[0], LANES), F32),
             pltpu.VMEM((2 * latent.shape[0], channels), F32),
+            pltpu.VMEM(mix_weight.shape, BF16),
+            pltpu.VMEM((pl.cdiv(count, PACK), PACK_ROWS, LANES), BF16),
             pltpu.VMEM((WORKERS, 8, LANES), BF16),
             pltpu.VMEM((4, lons, 8, LANES), BF16),
             pltpu.VMEM((2, lons, 8, LANES), BF16),
             pltpu.VMEM((WORKERS, 8, LANES), BF16),
-            pltpu.VMEM((8 * lons, LANES), F32),
-            pltpu.VMEM((4 * lons, LANES), F32),
-            pltpu.VMEM((8 * share, length), F32),
-            pltpu.VMEM((count * length, length), BF16),
+            pltpu.VMEM((4, WIDE, LANES), F32),
+            pltpu.VMEM((8 * share, GROUPS * WIDE), F32),
+            pltpu.VMEM((GROUPS * WIDE, length), BF16),
+            pltpu.VMEM((GROUPS * count * WIDE, length), BF16),
             pltpu.VMEM((share, LANES), F32),
             pltpu.VMEM((2, count * 2 * share, 2 * LANES), BF16),
+            pltpu.VMEM((4 * share, length), F32),
             pltpu.VMEM((2, length + 8, LANES), F32),
             pltpu.VMEM((2, length, LANES), F32),
-            pltpu.SemaphoreType.DMA((5,)),
+            pltpu.SemaphoreType.DMA((6,)),
             pltpu.SemaphoreType.DMA((2,)),
             pltpu.SemaphoreType.DMA((2,)),
             pltpu.SemaphoreType.DMA,
             pltpu.SemaphoreType.DMA,
             pltpu.SemaphoreType.DMA,
-            pltpu.SemaphoreType.DMA((4,)),
+            pltpu.SemaphoreType.DMA((4, GROUPS)),
             pltpu.SemaphoreType.DMA((2,)),
             pltpu.SemaphoreType.DMA,
         ],

time: 26.2 us -> 25.2 us (0.962)
  the two profiles are of different devices: /device:TPU:25 before, /device:TPU:49 now
where the time goes in v6:
time: 25.2 us; the launch traced here: 25 us
  Pallas kernels  24.4 us (97%)
  local copies, waits for them, and re-layouts  0.61 us (2%)
    pallas_call x1, Pallas kernels, local(): pl.pallas_call(kernel, out_shape=jax.ShapeDtypeStruct(latent.shape, laten...  24.4 us
    unnamed x1, local copies, waits for them, and re-layouts  0.61 us

profile of v6, /device:TPU:49, one launch (start us, length us, event | category | flops | bytes accessed | tf_op | source)
XLA Modules:
  0.0 25.0 jit_solution(12984949070148441599)
XLA Ops:
  0.0 24.4 %shard_map.64 = bf16[12,2,640]{2,1,0:T(2,128)(2,1)S(1)} custom-call(bf16[12,2,640]{2,1,0:T(2,128)(2,1)} %bitcast.4, bf16[9,384]{1,0:T(8,128)(2,1)} %filter_hbm.1, bf16[9,20,20]{2,1,0:T(8,128)(2,1)} %mix_hbm.1, bf16[3,2,9]{2,1,0:T(2,128)(2,1)} %bitcast.5, bf16[640,1280]{1,0:T(8,128)(2,1)} %up_hbm.1, bf16[1280,640]{1,0:T(8,128)(2,1)} %down_hbm.1), custom_call_target="tpu_custom_call" | custom-call | tf_op jit(solution)/shard_map/pallas_call | solution.py:462
  24.4 0.6 %copy.8 = bf16[2,12,640]{2,0,1:T(2,128)(2,1)} copy(bf16[2,12,640]{2,0,1:T(2,128)(2,1)S(1)} %bitcast.3) | data formatting | bytes 61440

commit v7 on v6

--- a/solution.py
+++ b/solution.py
@@ -11,6 +11,7 @@
 X_CHIPS, Z_CHIPS = 4, 8
 WORK_Z = 2
 WORKERS = X_CHIPS * WORK_Z * 2
+SIGNAL_Z = (4, 5, 6, 7, 3, 2, 1, 0)
 WORK_AT = [(core, x * Z_CHIPS + z) for x in range(X_CHIPS) for z in range(WORK_Z) for core in range(2)]
 LANES = 128
 AHEAD = 8
@@ -82,7 +83,7 @@
 
     @pl.when(works)
     def _():
-        for z in reversed(range(Z_CHIPS)):
+        for z in SIGNAL_Z:
             for x in range(X_CHIPS):
                 to_lon = x * Z_CHIPS + z
                 for c in range(2):
@@ -94,15 +95,13 @@
                     else:
                         signal(base + c, to_lon)
 
-        @pl.when(has_high)
-        def _():
-            for z in reversed(range(Z_CHIPS)):
+            @pl.when(has_high)
+            def _(z=z):
                 for x in range(X_CHIPS):
                     signal(base + 2, x * Z_CHIPS + z)
 
-        @pl.when(has_low)
-        def _():
-            for z in reversed(range(Z_CHIPS)):
+            @pl.when(has_low)
+            def _(z=z):
                 for x in range(X_CHIPS):
                     signal(base - 1, x * Z_CHIPS + z)
 
@@ -166,11 +165,31 @@
     def _():
         parts_in[core + 1, my_place] = parts_out[my_work]
 
-    @pl.when(has_side)
-    def _():
-        slot = jnp.where(core == 0, 3, 0)
-        for w, (c, to_lon) in enumerate(WORK_AT):
-            send(parts_out.at[w], parts_in.at[slot, my_place], side_sem, in_sem.at[slot, my_group], (aside + c, to_lon)).start()
+    def send_points(steps):
+        for side, z, dx in steps:
+            to_x = lax.rem(my_x + dx, X_CHIPS)
+            to_lon = to_x * Z_CHIPS + z
+            for c in range(2):
+                w = (to_x * WORK_Z + z) * 2 + c
+                if side:
+
+                    @pl.when(has_side)
+                    def _(c=c, w=w, to_lon=to_lon):
+                        slot = jnp.where(core == 0, 3, 0)
+                        send(
+                            parts_out.at[w], parts_in.at[slot, my_place], side_sem, in_sem.at[slot, my_group], (aside + c, to_lon)
+                        ).start()
+                else:
+
+                    @pl.when((lon != to_lon) | (core != c))
+                    def _(c=c, w=w, to_lon=to_lon):
+                        send(
+                            parts_out.at[w], parts_in.at[core + 1, my_place], out_sem, in_sem.at[core + 1, my_group], (base + c, to_lon)
+                        ).start()
+
+    steps = [(side, z, dx) for side in (1, 0) for z in reversed(range(WORK_Z)) for dx in (2, 1, 3, 0)]
+    steps.sort(key=lambda s: -(s[0] + s[1] + min(s[2], X_CHIPS - s[2])))
+    send_points(steps[: len(steps) // 2])
 
     @pl.when(core == 1)
     def _():
@@ -191,14 +210,7 @@
     def _():
         mix_copy.start()
 
-    for w, (c, to_lon) in enumerate(WORK_AT):
-
-        @pl.when((lon != to_lon) | (core != c))
-        def _(w=w, c=c, to_lon=to_lon):
-            send(
-                parts_out.at[w], parts_in.at[core + 1, my_place], out_sem, in_sem.at[core + 1, my_group], (base + c, to_lon)
-            ).start()
-
+    send_points(steps[len(steps) // 2 :])
     up_load.start()
     down_load.start()
     filter_load.wait()

time: 25.2 us -> 24.8 us (0.984)
  Pallas kernels: 24.4 us -> 24 us
    pallas_call x1, Pallas kernels: 24.4 us -> 24 us  [local(): pl.pallas_call(kernel, out_shape=jax.ShapeDtypeStruct(latent.shape, laten...]
where the time goes in v7:
time: 24.8 us; the launch traced here: 24.7 us
  Pallas kernels  24 us (97%)
  local copies, waits for them, and re-layouts  0.61 us (2%)
    pallas_call x1, Pallas kernels, local(): pl.pallas_call(kernel, out_shape=jax.ShapeDtypeStruct(latent.shape, laten...  24 us
    unnamed x1, local copies, waits for them, and re-layouts  0.61 us

profile of v7, /device:TPU:49, one launch (start us, length us, event | category | flops | bytes accessed | tf_op | source)
XLA Modules:
  0.0 24.7 jit_solution(18003734418328371005)
XLA Ops:
  0.0 24.0 %shard_map.64 = bf16[12,2,640]{2,1,0:T(2,128)(2,1)S(1)} custom-call(bf16[12,2,640]{2,1,0:T(2,128)(2,1)} %bitcast.4, bf16[9,384]{1,0:T(8,128)(2,1)} %filter_hbm.1, bf16[9,20,20]{2,1,0:T(8,128)(2,1)} %mix_hbm.1, bf16[3,2,9]{2,1,0:T(2,128)(2,1)} %bitcast.5, bf16[640,1280]{1,0:T(8,128)(2,1)} %up_hbm.1, bf16[1280,640]{1,0:T(8,128)(2,1)} %down_hbm.1), custom_call_target="tpu_custom_call" | custom-call | tf_op jit(solution)/shard_map/pallas_call | solution.py:474
  24.0 0.6 %copy.8 = bf16[2,12,640]{2,0,1:T(2,128)(2,1)} copy(bf16[2,12,640]{2,0,1:T(2,128)(2,1)S(1)} %bitcast.3) | data formatting | bytes 61440

commit v8 on v7

--- a/solution.py
+++ b/solution.py
@@ -199,7 +199,8 @@
             packed = jnp.zeros((share, LANES), F32)
             for n in range(min(PACK, count - first)):
                 mix_wide[0:group, 0:group] = mix_own[first + n].astype(F32)
-                packed = packed + (pltpu.roll(mix_wide[...], group * n, 1) if n else mix_wide[...])
+                once = mix_wide[0:share, :]
+                packed = packed + (pltpu.roll(once, group * n, 1) if n else once)
             mix_out[first // PACK] = packed[0:PACK_ROWS].astype(BF16)
 
     @pl.when(mix_away)
@@ -333,7 +334,7 @@
                 once = pltpu.roll(once, shift, 1) if shift else once
                 once = jnp.where((wide_lane >= group * h) & (wide_lane < group * (h + 1)), once, 0.0)
                 mix_wide[group * h : group * (h + 1), :] = once[0:group]
-            once = mix_wide[...]
+            once = mix_wide[0:share, :]
             every = once + pltpu.roll(once, share, 1) + pltpu.roll(once, 2 * share, 1)
             for o in range(2):
                 scaled = []
@@ -422,7 +423,7 @@
                 sums[q][tile + 1] = jnp.where(lane < place + share - LANES, piece, sums[q][tile + 1])
     returned_rows = jnp.concatenate([jnp.concatenate(one, axis=1) for one in sums], axis=0)
 
-    summed = (rows[...] + returned_rows).astype(BF16).astype(F32)
+    summed = (rows[0 : 2 * width, :] + returned_rows).astype(BF16).astype(F32)
     mean = jnp.mean(summed, axis=1, keepdims=True)
     centred = summed - mean
     var = jnp.mean(centred * centred, axis=1, keepdims=True)
@@ -483,8 +484,8 @@
             pltpu.VMEM((2, *band_weight.shape), BF16),
             pltpu.VMEM(w_up.shape, BF16),
             pltpu.VMEM(w_down.shape, BF16),
-            pltpu.VMEM((channels // LANES, 2 * latent.shape[0], LANES), F32),
-            pltpu.VMEM((2 * latent.shape[0], channels), F32),
+            pltpu.VMEM((channels // LANES, 2 * latent.shape[0] + 8, LANES), F32),
+            pltpu.VMEM((2 * latent.shape[0] + 8, channels), F32),
             pltpu.VMEM(mix_weight.shape, BF16),
             pltpu.VMEM((pl.cdiv(count, PACK), PACK_ROWS, LANES), BF16),
             pltpu.VMEM((WORKERS, 8, LANES), BF16),
@@ -495,7 +496,7 @@
             pltpu.VMEM((8 * share, GROUPS * WIDE), F32),
             pltpu.VMEM((GROUPS * WIDE, length), BF16),
             pltpu.VMEM((GROUPS * count * WIDE, length), BF16),
-            pltpu.VMEM((share, LANES), F32),
+            pltpu.VMEM((share + 8, LANES), F32),
             pltpu.VMEM((2, count * 2 * share, 2 * LANES), BF16),
             pltpu.VMEM((4 * share, length), F32),
             pltpu.VMEM((2, length + 8, LANES), F32),

time: 24.8 us -> 24.8 us (level)
  no operation moved by 1% of the time
where the time goes in v8:
time: 24.8 us; the launch traced here: 24.6 us
  Pallas kernels  24 us (97%)
  local copies, waits for them, and re-layouts  0.61 us (2%)
    pallas_call x1, Pallas kernels, local(): pl.pallas_call(kernel, out_shape=jax.ShapeDtypeStruct(latent.shape, laten...  24 us
    unnamed x1, local copies, waits for them, and re-layouts  0.61 us

profile of v8, /device:TPU:49, one launch (start us, length us, event | category | flops | bytes accessed | tf_op | source)
XLA Modules:
  0.0 24.6 jit_solution(15392948667521665853)
XLA Ops:
  0.0 24.0 %shard_map.64 = bf16[12,2,640]{2,1,0:T(2,128)(2,1)S(1)} custom-call(bf16[12,2,640]{2,1,0:T(2,128)(2,1)} %bitcast.4, bf16[9,384]{1,0:T(8,128)(2,1)} %filter_hbm.1, bf16[9,20,20]{2,1,0:T(8,128)(2,1)} %mix_hbm.1, bf16[3,2,9]{2,1,0:T(2,128)(2,1)} %bitcast.5, bf16[640,1280]{1,0:T(8,128)(2,1)} %up_hbm.1, bf16[1280,640]{1,0:T(8,128)(2,1)} %down_hbm.1), custom_call_target="tpu_custom_call" | custom-call | tf_op jit(solution)/shard_map/pallas_call | solution.py:475
  24.0 0.6 %copy.8 = bf16[2,12,640]{2,0,1:T(2,128)(2,1)} copy(bf16[2,12,640]{2,0,1:T(2,128)(2,1)S(1)} %bitcast.3) | data formatting | bytes 61440
